TPU v7x, 32 devices: a whole 2x2x4 slice. The times are simulated.
32 devices in a mesh: row: 8 (over z, y), col: 4 (over x, core).
Axes of the slice: x: 2, y: 2, z: 4, core: 2. Of those that a mesh axis runs over, the one named last changes fastest.
Arguments:
- obs_panel: bfloat16 [196608, 2048], P('row', 'col'), may hold values from -0.1875 to 0.1875
- skies: bfloat16 [196608, 256], P('row', 'col'), may hold values from -6 to 6
- panel_index: int32 [2048], replicated, may hold values from 0 to 196607
- prior_sum: float32 [196608, 256], P('row', 'col'), may hold values from -6 to 6
- apod: float32 [196608], P('row'), may hold values from 0.05 to 1
- proj_panel: bfloat16 [2048, 196608], P(None, ('row', 'col')), may hold values from -0.02734375 to 0.02734375
Outputs:
- reobserved: float32 [196608, 256], P('row', 'col')
- projection: float32 [2048, 256], P('row', 'col')
Inputs may be any that keep to these rules, and one draw needn't show every extreme that they name: `panel_index`: rows of the observed patch; a row may appear more than once.
All inputs are finite; a program needn't handle non-finite values.
Results may differ from a plain program's by a relative error of at most 0.0029.
Values may be sent and summed in bfloat16 or wider, within the bound.
A program may use at most 192 MiB of HBM per device.

v0:
```python
import functools
import math

import jax
import jax.numpy as jnp
from jax import lax
from jax.experimental import pallas as pl
from jax.experimental.pallas import tpu as pltpu
from jax.sharding import PartitionSpec as P

MESH = pl.DeviceIdType.MESH
NT = (((1,), (1,)), ((), ()))
UNIT = 256
D2, D3, D4 = 1, 3, 5
LIMIT = 48 * 1024 * 1024


def remote(src, dst, send, recv, row, col):
    return pltpu.make_async_remote_copy(
        src_ref=src, dst_ref=dst, send_sem=send, recv_sem=recv, device_id=(row, col), device_id_type=MESH
    )


def meet(devices):
    barrier = pltpu.get_barrier_semaphore()
    for device in devices:
        pl.semaphore_signal(barrier, inc=1, device_id=device, device_id_type=MESH)
    pl.semaphore_wait(barrier, len(devices))


def meet_all(n_row, n_col):
    barrier = pltpu.get_barrier_semaphore()
    me = lax.axis_index("row") * n_col + lax.axis_index("col")
    every = n_row * n_col

    def tell(i, carry):
        to = lax.rem(me + i, every)
        pl.semaphore_signal(barrier, inc=1, device_id=(lax.div(to, n_col), lax.rem(to, n_col)), device_id_type=MESH)
        return carry

    lax.fori_loop(1, every, tell, 0)
    pl.semaphore_wait(barrier, every - 1)


def spread_kernel(n_row, n_col, own_ref, out_ref, land, mine, gather, send1, recv1, send2, recv2):
    r, c = lax.axis_index("row"), lax.axis_index("col")
    meet_all(n_row, n_col)
    sims, panel = own_ref.shape
    part = panel // n_row
    rep = n_row // n_col

    def part_of(row):
        return lax.rem(row, 2) * (n_row // 2) + lax.div(row, 2)

    first = []
    for d in range(1, n_row):
        to = lax.rem(r + d, n_row)
        cp = remote(own_ref.at[:, pl.ds(pl.multiple_of(part_of(to) * part, part), part)], land.at[d - 1],
                    send1.at[d - 1], recv1.at[d - 1], to, c)
        cp.start()
        first.append(cp)
    total = own_ref[:, pl.ds(pl.multiple_of(part_of(r) * part, part), part)].astype(jnp.float32)
    for d in range(1, n_row):
        first[d - 1].wait_recv()
        total = total + land[d - 1].astype(jnp.float32)
    mine[...] = total.astype(mine.dtype)
    sub = lax.rem(part_of(r), rep)
    col_to = lax.div(part_of(r), rep)
    slot = sub * n_col + c
    second = []
    for d in range(n_row):
        to = lax.rem(r + d, n_row)
        cp = remote(mine, gather.at[slot], send2.at[d], recv2.at[slot], to, col_to)
        second.append(cp)
        if d > 0:
            cp.start()
        else:
            @pl.when(col_to != c)
            def _():
                cp.start()

            @pl.when(col_to == c)
            def _():
                gather[slot] = mine[...]
    for s in range(rep):
        for j in range(n_col):
            here = (c * rep + s == part_of(r)) & (c == j)

            @pl.when(jnp.logical_not(here))
            def _():
                remote(mine, gather.at[s * n_col + j], send2.at[0], recv2.at[s * n_col + j], r, c).wait_recv()
    chips = n_col // 2
    core, chip = lax.rem(c, 2), lax.div(c, 2)
    for q in range(n_col):
        other, shift = q // chips, q % chips
        source = lax.rem(chip + shift, chips) * 2 + (core if other == 0 else 1 - core)
        for s in range(rep):
            out_ref[q * sims:(q + 1) * sims, s * part:(s + 1) * part] = gather[s * n_col + source]
    for cp in first:
        cp.wait_send()
    for d in range(n_row):
        if d > 0:
            second[d].wait_send()
        else:
            @pl.when(col_to != c)
            def _():
                second[0].wait_send()


def spread(own, n_row, n_col):
    sims, panel = own.shape
    part = panel // n_row
    vmem = pl.BlockSpec(memory_space=pltpu.VMEM)
    return pl.pallas_call(
        functools.partial(spread_kernel, n_row, n_col),
        out_shape=jax.ShapeDtypeStruct((sims * n_col, panel // n_col), own.dtype),
        in_specs=[vmem],
        out_specs=vmem,
        scratch_shapes=[
            pltpu.VMEM((n_row - 1, sims, part), own.dtype),
            pltpu.VMEM((sims, part), own.dtype),
            pltpu.VMEM((n_row, sims, part), own.dtype),
            pltpu.SemaphoreType.DMA((n_row - 1,)),
            pltpu.SemaphoreType.DMA((n_row - 1,)),
            pltpu.SemaphoreType.DMA((n_row,)),
            pltpu.SemaphoreType.DMA((n_row,)),
        ],
        compiler_params=pltpu.CompilerParams(has_side_effects=True, collective_id=0, vmem_limit_bytes=LIMIT),
        name="spread",
    )(own)


def fold_kernel(n_row, n_col, acc_ref, swapped_ref, out_ref, sa, lx0, b0, ly0, ly1, b1, lx1, ends, lz,
                sx0, rx0, sy, ry, sx1, rx1, sz, rz):
    r, c = lax.axis_index("row"), lax.axis_index("col")
    chips, pairs = n_col // 2, n_row // 2
    core, chip = lax.rem(c, 2), lax.div(c, 2)
    low, high = lax.rem(r, 2), lax.div(r, 2)
    beside = high * 2 + 1 - low
    meet([(r, lax.rem(chip + s, chips) * 2 + core) for s in range(1, chips)]
         + [(beside, c)] + [(lax.rem(high + d, pairs) * 2 + low, c) for d in range(1, pairs)])
    sims, pb = out_ref.shape
    hs, half = sims // 2, pairs * pb

    def side(which):
        return pl.ds(pl.multiple_of(which * half, half), half)

    def to_col(s):
        return lax.rem(chip + s, chips) * 2 + core

    copies = []

    def go(*args):
        cp = remote(*args)
        cp.start()
        copies.append(cp)
        return cp

    order = list(range(1, chips)) + [0]
    x0 = []
    for s in order:
        mine = (chips - s) % chips
        theirs = lax.rem(2 * chips - s - core, chips)
        for k in range(n_row):
            from_lanes = slice(k * pb, (k + 1) * pb)
            at = (k % 2) * half + (k // 2) * pb
            for h in range(2):
                rows = slice(h * hs, (h + 1) * hs)
                sa[h, s, :, at:at + pb] = acc_ref[mine, rows, from_lanes] + swapped_ref[theirs, rows, from_lanes]
        if s > 0:
            x0.append(go(sa.at[0, s], lx0.at[s - 1], sx0.at[s - 1], rx0.at[s - 1], r, to_col(s)))
    y1 = go(sa.at[1, :, :, side(1 - low)], ly1, sy.at[1], ry.at[1], beside, c)
    total = sa[0, 0]
    for s in range(1, chips):
        x0[s - 1].wait_recv()
        total = total + lx0[s - 1]
    b0[...] = total
    y0 = go(b0.at[:, side(1 - low)], ly0, sy.at[0], ry.at[0], beside, c)
    y1.wait_recv()
    b1[...] = sa[1, :, :, side(low)] + ly1[...]
    x1 = [go(b1.at[s], lx1.at[s - 1], sx1.at[s - 1], rx1.at[s - 1], r, to_col(s)) for s in range(1, chips)]
    z = []
    for h in range(2):
        if h == 0:
            y0.wait_recv()
            ends[0] = b0[:, side(low)] + ly0[...]
        else:
            total = b1[0]
            for s in range(1, chips):
                x1[s - 1].wait_recv()
                total = total + lx1[s - 1]
            ends[1] = total
        for d in range(1, pairs):
            to = lax.rem(high + d, pairs)
            z.append(go(ends.at[h, :, pl.ds(pl.multiple_of(to * pb, pb), pb)], lz.at[h, d - 1], sz.at[h, d - 1], rz.at[h, d - 1], to * 2 + low, c))
    for h in range(2):
        total = ends[h, :, pl.ds(pl.multiple_of(high * pb, pb), pb)]
        for d in range(1, pairs):
            z[h * (pairs - 1) + d - 1].wait_recv()
            total = total + lz[h, d - 1]
        out_ref[h * hs:(h + 1) * hs, :] = total
    for cp in copies:
        cp.wait_send()


def fold(acc, swapped, n_row, n_col):
    _, sims, prows = acc.shape
    chips, pairs = n_col // 2, n_row // 2
    hs, pb, half = sims // 2, prows // n_row, prows // 2
    vmem = pl.BlockSpec(memory_space=pltpu.VMEM)
    dma = pltpu.SemaphoreType.DMA

    def f32(*shape):
        return pltpu.VMEM(shape, jnp.float32)

    return pl.pallas_call(
        functools.partial(fold_kernel, n_row, n_col),
        out_shape=jax.ShapeDtypeStruct((sims, pb), jnp.float32),
        in_specs=[vmem] * 2,
        out_specs=vmem,
        scratch_shapes=[
            f32(2, chips, hs, prows), f32(chips - 1, hs, prows), f32(hs, prows), f32(hs, half),
            f32(chips, hs, half), f32(chips, hs, half), f32(chips - 1, hs, half), f32(2, hs, half), f32(2, pairs - 1, hs, pb),
            dma((chips - 1,)), dma((chips - 1,)), dma((2,)), dma((2,)),
            dma((chips - 1,)), dma((chips - 1,)), dma((2, pairs - 1)), dma((2, pairs - 1)),
        ],
        compiler_params=pltpu.CompilerParams(has_side_effects=True, collective_id=1, vmem_limit_bytes=LIMIT),
        name="fold",
    )(acc, swapped)


def stream_kernel(n_col, units, p_ref, o_ref, *refs):
    priors, (apod_ref, proj_ref) = refs[:n_col], refs[n_col:n_col + 2]
    re_ref, *accs = refs[n_col + 2:n_col + 5]
    keep, swap, near, fars, far, ws, wr, ss, sr, fs, fr, gs, gr = refs[n_col + 5:]
    r, c = lax.axis_index("row"), lax.axis_index("col")
    chips = n_col // 2
    core, chip = lax.rem(c, 2), lax.div(c, 2)
    sims, size = wr.shape[2:]
    g = pl.program_id(0)

    def near_copy(u):
        k, q = lax.rem(u, swap.shape[0]), lax.rem(u, near.shape[0])
        return remote(swap.at[k], near.at[q], ss.at[k], sr.at[q], r, chip * 2 + 1 - core)

    def far_copies(u):
        k, q = lax.rem(u, fars.shape[0]), lax.rem(u, far.shape[0])
        return [remote(fars.at[k, s], far.at[q, s], fs.at[k, s], fr.at[q, s], r, lax.rem(chip + s + 1, chips) * 2 + core)
                for s in range(chips - 1)]

    def weighted_copies(u):
        k, q = lax.rem(u, ws.shape[0]), lax.rem(u, wr.shape[0])
        return [remote(ws.at[k, d], wr.at[q, d - 1], gs.at[k, d - 1], gr.at[q, d - 1], r, lax.rem(c + d, n_col))
                for d in range(1, n_col)]

    @pl.when(g == 0)
    def _():
        meet([(r, lax.rem(c + d, n_col)) for d in range(1, n_col)])
        for acc in accs:
            acc[...] = jnp.zeros_like(acc)

    @pl.when((g >= D2) & (g < units + D2))
    def _():
        u = g - D2
        near_copy(u).wait_recv()

        @pl.when(u >= fars.shape[0])
        def _():
            for cp in far_copies(u - fars.shape[0]):
                cp.wait_send()

        k, q, e = lax.rem(u, fars.shape[0]), lax.rem(u, near.shape[0]), lax.rem(u, keep.shape[0])
        copies = far_copies(u)
        for s in range(chips - 1):
            away = slice((s + 1) * sims, (s + 2) * sims)
            fars[k, s] = (keep[e, away] + near[q, away].astype(jnp.float32)).astype(jnp.bfloat16)
            copies[s].start()
        keep[e, :sims] = keep[e, :sims] + near[q, :sims].astype(jnp.float32)

    @pl.when((g >= D3) & (g < units + D3))
    def _():
        u = g - D3
        for cp in far_copies(u):
            cp.wait_recv()

        @pl.when(u >= ws.shape[0])
        def _():
            for cp in weighted_copies(u - ws.shape[0]):
                cp.wait_send()

        k, q, e = lax.rem(u, ws.shape[0]), lax.rem(u, far.shape[0]), lax.rem(u, keep.shape[0])
        for i in range(n_col):
            lanes = slice(i * size, (i + 1) * size)
            total = keep[e, :sims, lanes]
            for s in range(chips - 1):
                total = total + far[q, s, :, lanes].astype(jnp.float32)
            total = priors[i][...] + total
            re_ref[i] = total
            ws[k, lax.rem(i - c + n_col, n_col)] = (apod_ref[i:i + 1, :] * total).astype(jnp.bfloat16)
        for cp in weighted_copies(u):
            cp.start()

    @pl.when(g < units)
    def _():
        k, e = lax.rem(g, swap.shape[0]), lax.rem(g, keep.shape[0])

        @pl.when(g >= swap.shape[0])
        def _():
            near_copy(g - swap.shape[0]).wait_send()

        kept = n_col * sims // 2
        rows = o_ref[...].reshape(n_col * size, o_ref.shape[2])
        value = lax.dot_general(p_ref[...], rows, NT, preferred_element_type=jnp.float32)
        swap[k] = value[kept:].astype(jnp.bfloat16)
        near_copy(g).start()
        keep[e] = value[:kept]

    @pl.when(g >= D4)
    def _():
        u = g - D4
        for cp in weighted_copies(u):
            cp.wait_recv()
        k, q = lax.rem(u, ws.shape[0]), lax.rem(u, wr.shape[0])
        w = jnp.concatenate([ws[k, 0]] + [wr[q, d] for d in range(n_col - 1)], axis=0)
        prows = proj_ref.shape[0]
        tile = min(512, prows)
        for j in range(0, prows, tile):
            value = lax.dot_general(w, proj_ref[j:j + tile, :], NT, preferred_element_type=jnp.float32)
            for d in range(n_col):
                accs[d % 2][d // 2, :, j:j + tile] += value[d * sims:(d + 1) * sims]

    @pl.when(g == units + D4 - 1)
    def _():
        for b in range(min(units, swap.shape[0])):
            near_copy(units - 1 - b).wait_send()
        for b in range(min(units, fars.shape[0])):
            for cp in far_copies(units - 1 - b):
                cp.wait_send()
        for b in range(min(units, ws.shape[0])):
            for cp in weighted_copies(units - 1 - b):
                cp.wait_send()


def stream(picked, obs, prior, apod, proj, n_col):
    depth, (sims, rows), prows = obs.shape[1], prior.shape, proj.shape[0]
    slab = rows // n_col
    units = slab // math.gcd(slab, UNIT)
    size = slab // units
    kept = n_col * sims // 2
    chips = n_col // 2

    def at(g, lag):
        return jnp.clip(g - lag, 0, units - 1)

    n_near, n_far, n_got = 2 * D2, 2 * D3 + 2 - 2 * D2, 2 * D4 + 2 - 2 * D3
    n_ws = D4 - D3 + 2
    wide = n_col * size
    dma, bf16 = pltpu.SemaphoreType.DMA, jnp.bfloat16
    prior_specs = [pl.BlockSpec((sims, size), functools.partial(lambda g, i: (0, i * units + at(g, D3)), i=i)) for i in range(n_col)]
    return pl.pallas_call(
        functools.partial(stream_kernel, n_col, units),
        grid=(units + D4,),
        in_specs=[
            pl.BlockSpec(picked.shape, lambda g: (0, 0)),
            pl.BlockSpec((n_col, size, depth), lambda g: (0, at(g, 0), 0)),
            *prior_specs,
            pl.BlockSpec((n_col, size), lambda g: (0, at(g, D3))),
            pl.BlockSpec((prows, size), lambda g: (0, at(g, D4))),
        ],
        out_specs=[
            pl.BlockSpec((n_col, sims, size), lambda g: (0, 0, at(g, D3))),
            *[pl.BlockSpec((chips, sims, prows), lambda g: (0, 0, 0))] * 2,
        ],
        out_shape=[
            jax.ShapeDtypeStruct((n_col, sims, slab), jnp.float32),
            *[jax.ShapeDtypeStruct((chips, sims, prows), jnp.float32)] * 2,
        ],
        scratch_shapes=[
            pltpu.VMEM((D3 + 1, kept, wide), jnp.float32),
            pltpu.VMEM((2, kept, wide), bf16),
            pltpu.VMEM((n_near, kept, wide), bf16),
            pltpu.VMEM((2, chips - 1, sims, wide), bf16),
            pltpu.VMEM((n_far, chips - 1, sims, wide), bf16),
            pltpu.VMEM((n_ws, n_col, sims, size), bf16),
            pltpu.VMEM((n_got, n_col - 1, sims, size), bf16),
            dma((2,)), dma((n_near,)), dma((2, chips - 1)), dma((n_far, chips - 1)),
            dma((n_ws, n_col - 1)), dma((n_got, n_col - 1)),
        ],
        compiler_params=pltpu.CompilerParams(has_side_effects=True, collective_id=2, vmem_limit_bytes=LIMIT, dimension_semantics=("arbitrary",)),
        name="stream",
    )(picked, obs.reshape(n_col, slab, depth), *[prior] * n_col, apod.reshape(n_col, slab), proj)


def on_device(n_row, n_col, obs_panel, skies, panel_index, prior_sum, apod, proj_panel):
    rows_blk, sims = skies.shape
    local_idx = panel_index - lax.axis_index("row") * rows_blk
    inside = (local_idx >= 0) & (local_idx < rows_blk)
    taken = jnp.take(skies, jnp.clip(local_idx, 0, rows_blk - 1), axis=0)
    own = jnp.where(inside[:, None], taken, jnp.zeros((), jnp.bfloat16)).T
    picked = spread(own, n_row, n_col)

    out, acc, other = stream(picked, obs_panel, prior_sum.T, apod, proj_panel, n_col)
    swapped = lax.ppermute(other, "col", [(i, i ^ 1) for i in range(n_col)])
    projection = fold(acc, swapped, n_row, n_col)
    return out.transpose(0, 2, 1).reshape(rows_blk, sims), projection.T


def solution(mesh):
    in_specs = (P("row", "col"), P("row", "col"), P(), P("row", "col"), P("row"), P(None, ("row", "col")))
    out_specs = (P("row", "col"), P("row", "col"))
    body = functools.partial(on_device, mesh.shape["row"], mesh.shape["col"])
    return jax.shard_map(body, mesh=mesh, in_specs=in_specs, out_specs=out_specs, check_vma=False)
```

profile of v0, /device:TPU:0, one launch (start us, length us, event | category | flops | bytes accessed | tf_op | source)
XLA Modules:
  0.0 176.7 jit_solution(12890829769469435124)
XLA Ops:
  0.6 0.7 compare_and_fusion.1
  1.3 0.7 fusion
  2.1 0.0 copy-start
  2.1 6.6 %copy.10 = bf16[24576,64]{1,0:T(8,128)(2,1)} copy(bf16[24576,64]{0,1:T(8,128)(2,1)} %param.7) | data formatting | bytes 6291456 | tf_op args[1]
  8.6 9.2 %gather_fusion = bf16[2048,64]{1,0:T(8,128)(2,1)S(1)} fusion(bf16[24576,64]{1,0:T(8,128)(2,1)} %copy.10, s32[2048]{0:T(1024)S(1)} %fusion), kind=kCustom, calls=%fused_computation | custom fusion | bytes 532480 | tf_op jit(solution)/shard_map/jit(_take)/gather | solution.py:398
  17.8 0.2 copy.11
  18.1 19.3 %spread.1.p_ref = bf16[256,512]{1,0:T(8,128)(2,1)S(1)} custom-call(bf16[64,2048]{1,0:T(8,128)(2,1)S(1)} %select_bitcast_fusion.own_ref), custom_call_target="tpu_custom_call" | custom-call | tf_op jit(solution)/shard_map/spread/pallas_call | solution.py:114
  37.4 0.0 copy-done
  37.4 110.7 %stream.1 = (f32[4,64,6144]{2,1,0:T(8,128)}, f32[2,64,2048]{2,1,0:T(8,128)S(1)}, f32[2,64,2048]{2,1,0:T(8,128)S(1)}) custom-call(bf16[256,512]{1,0:T(8,128)(2,1)S(1)} %spread.1.p_ref, bf16[4,6144,512]{2,1,0:T(8,128)(2,1)} %bitcast.13, f32[64,24576]{1,0:T(8,128)} %bitcast.9, f32[64,24576]{1,0:T(8,128)} %bitcast.10, f32[64,24576]{1,0:T(8,128)} %bitcast.11, ...), custom_call_target="tpu_custom_call" | custom-call | tf_op jit(solution)/shard_map/stream/pallas_call | solution.py:360
  148.1 0.2 collective-permute-start
  148.3 6.2 %copy.13 = f32[4,8,8,6144]{3,2,0,1:T(8,128)} copy(f32[4,8,8,6144]{3,2,1,0:T(8,128)} %bitcast.15) | data formatting | bytes 12582912 | tf_op jit(solution)/shard_map/reshape | solution.py:405
  154.5 0.0 collective-permute-done.swapped_ref
  154.5 21.5 %fold.1 = f32[64,256]{1,0:T(8,128)S(1)} custom-call(f32[2,64,2048]{2,1,0:T(8,128)S(1)} %get-tuple-element.6.acc_ref, f32[2,64,2048]{2,1,0:T(8,128)S(1)} %collective-permute-done.swapped_ref), custom_call_target="tpu_custom_call" | custom-call | tf_op jit(solution)/shard_map/fold/pallas_call | solution.py:216
  176.0 0.6 copy.15
  (2 shorter events, 0.1 us)
Async XLA Ops:
  2.1 35.3 %copy-start = (f32[24576]{0:T(1024)S(1)}, f32[24576]{0:T(1024)}, u32[]{:S(2)}) copy-start(f32[24576]{0:T(1024)} %param.10) | copy-start | bytes 294916
  148.1 6.4 %collective-permute-start = (f32[2,64,2048]{2,1,0:T(8,128)S(1)}, f32[2,64,2048]{2,1,0:T(8,128)S(1)}, u32[]{:S(2)}, u32[]{:S(2)}) collective-permute-start(f32[2,64,2048]{2,1,0:T(8,128)S(1)} %get-tuple-element.7), channel_id=1, source_target_pairs={{0,1},{1,0},{2,3},{3,2},{4,5},{5,4},{6,7},{7,6},{8,9},{9,8},{10,11... | collective-permute-start | bytes 3145736 | tf_op jit(solution)/shard_map/ppermute | solution.py:403
where the time goes:
time: 177 us
  Pallas kernels  151 us (85%)
  local copies, waits for them, and re-layouts  22.8 us (13%)
    pallas_call x1, Pallas kernels, stream(): pl.pallas_call(functools.partial(stream_kernel, n_col, units), grid=(unit...  111 us
    pallas_call x1, Pallas kernels, fold(): pl.pallas_call(functools.partial(fold_kernel, n_row, n_col), out_shape=ja...  21.5 us
    pallas_call x1, Pallas kernels, spread(): pl.pallas_call(functools.partial(spread_kernel, n_row, n_col), out_shape=...  19.3 us
    gather x2, local copies, waits for them, and re-layouts, on_device(): taken = jnp.take(skies, jnp.clip(local_idx, 0, rows_blk - 1), axis=0)  9.38 us
    unnamed x4, local copies, waits for them, and re-layouts  7.22 us
    reshape x1, local copies, waits for them, and re-layouts, on_device(): return (out.transpose(0, 2, 1).reshape(rows_blk, sims), projection.T)  6.17 us
  transfers between devices with their start and end apart: 1, of which 0 were waited for; matrix products, arithmetic and copies ran while one was open for 3% of the time, Pallas kernels for 0%

commit v1 on v0

v1 whole, which is shorter than its diff:
```python
import functools
import math

import jax
import jax.numpy as jnp
from jax import lax
from jax.experimental import pallas as pl
from jax.experimental.pallas import tpu as pltpu
from jax.sharding import PartitionSpec as P

MESH = pl.DeviceIdType.MESH
NT = (((1,), (1,)), ((), ()))
UNIT = 256
D2, D3 = 1, 4
IN, SENDS = 3, 3
LIMIT = 48 * 1024 * 1024


def remote(src, dst, send, recv, row, col):
    return pltpu.make_async_remote_copy(
        src_ref=src, dst_ref=dst, send_sem=send, recv_sem=recv, device_id=(row, col), device_id_type=MESH
    )


def meet(devices):
    barrier = pltpu.get_barrier_semaphore()
    for device in devices:
        pl.semaphore_signal(barrier, inc=1, device_id=device, device_id_type=MESH)
    pl.semaphore_wait(barrier, len(devices))


def meet_all(n_row, n_col):
    barrier = pltpu.get_barrier_semaphore()
    me = lax.axis_index("row") * n_col + lax.axis_index("col")
    every = n_row * n_col

    def tell(i, carry):
        to = lax.rem(me + i, every)
        pl.semaphore_signal(barrier, inc=1, device_id=(lax.div(to, n_col), lax.rem(to, n_col)), device_id_type=MESH)
        return carry

    lax.fori_loop(1, every, tell, 0)
    pl.semaphore_wait(barrier, every - 1)


def spread_kernel(n_row, n_col, own_ref, out_ref, land, mine, gather, send1, recv1, send2, recv2):
    r, c = lax.axis_index("row"), lax.axis_index("col")
    meet_all(n_row, n_col)
    sims, panel = own_ref.shape
    part = panel // n_row
    rep = n_row // n_col

    def part_of(row):
        return lax.rem(row, 2) * (n_row // 2) + lax.div(row, 2)

    first = []
    for d in range(1, n_row):
        to = lax.rem(r + d, n_row)
        cp = remote(own_ref.at[:, pl.ds(pl.multiple_of(part_of(to) * part, part), part)], land.at[d - 1],
                    send1.at[d - 1], recv1.at[d - 1], to, c)
        cp.start()
        first.append(cp)
    total = own_ref[:, pl.ds(pl.multiple_of(part_of(r) * part, part), part)].astype(jnp.float32)
    for d in range(1, n_row):
        first[d - 1].wait_recv()
        total = total + land[d - 1].astype(jnp.float32)
    mine[...] = total.astype(mine.dtype)
    sub = lax.rem(part_of(r), rep)
    col_to = lax.div(part_of(r), rep)
    slot = sub * n_col + c
    second = []
    for d in range(n_row):
        to = lax.rem(r + d, n_row)
        cp = remote(mine, gather.at[slot], send2.at[d], recv2.at[slot], to, col_to)
        second.append(cp)
        if d > 0:
            cp.start()
        else:
            @pl.when(col_to != c)
            def _():
                cp.start()

            @pl.when(col_to == c)
            def _():
                gather[slot] = mine[...]
    for s in range(rep):
        for j in range(n_col):
            here = (c * rep + s == part_of(r)) & (c == j)

            @pl.when(jnp.logical_not(here))
            def _():
                remote(mine, gather.at[s * n_col + j], send2.at[0], recv2.at[s * n_col + j], r, c).wait_recv()
    chips = n_col // 2
    core, chip = lax.rem(c, 2), lax.div(c, 2)
    for q in range(n_col):
        other, shift = q // chips, q % chips
        source = lax.rem(chip + shift, chips) * 2 + (core if other == 0 else 1 - core)
        for s in range(rep):
            out_ref[q * sims:(q + 1) * sims, s * part:(s + 1) * part] = gather[s * n_col + source]
    for cp in first:
        cp.wait_send()
    for d in range(n_row):
        if d > 0:
            second[d].wait_send()
        else:
            @pl.when(col_to != c)
            def _():
                second[0].wait_send()


def spread(own, n_row, n_col):
    sims, panel = own.shape
    part = panel // n_row
    vmem = pl.BlockSpec(memory_space=pltpu.VMEM)
    return pl.pallas_call(
        functools.partial(spread_kernel, n_row, n_col),
        out_shape=jax.ShapeDtypeStruct((sims * n_col, panel // n_col), own.dtype),
        in_specs=[vmem],
        out_specs=vmem,
        scratch_shapes=[
            pltpu.VMEM((n_row - 1, sims, part), own.dtype),
            pltpu.VMEM((sims, part), own.dtype),
            pltpu.VMEM((n_row, sims, part), own.dtype),
            pltpu.SemaphoreType.DMA((n_row - 1,)),
            pltpu.SemaphoreType.DMA((n_row - 1,)),
            pltpu.SemaphoreType.DMA((n_row,)),
            pltpu.SemaphoreType.DMA((n_row,)),
        ],
        compiler_params=pltpu.CompilerParams(has_side_effects=True, collective_id=0, vmem_limit_bytes=LIMIT),
        name="spread",
    )(own)


def stream_kernel(n_row, n_col, units, p_ref, apod_ref, obs, prior, proj, out_ref, pout_ref,
                  obs_v, pri_v, proj_v, near_s, near_r, keep, far_s, far_r, w_v, acc, g_s, g_r,
                  swap, fb, yb, gb, zb, hb, xb,
                  os, ps, js, ns, nr, fs, fr, ts, tr, us, ur, gs, gr, s1, r1, s2, r2, s3, r3, s4, r4):
    r, c = lax.axis_index("row"), lax.axis_index("col")
    chips, pairs = n_col // 2, n_row // 2
    core, chip = lax.rem(c, 2), lax.div(c, 2)
    low, high = lax.rem(r, 2), lax.div(r, 2)
    mate, beside = chip * 2 + 1 - core, high * 2 + 1 - low
    sims, rows = out_ref.shape
    prows, slab = proj.shape
    size, half = slab // units, chips * sims

    def other(t, same):
        return lax.rem(chip + t, chips) * 2 + (core if same else 1 - core)

    def span(q, u):
        return pl.ds(pl.multiple_of(q * slab + u * size, size), size)

    def loads(u):
        k, copies = lax.rem(u, IN), []
        for o in range(2):
            for t in range(chips):
                i, at = o * chips + t, span(other(t, o == 1), u)
                copies.append(pltpu.make_async_copy(obs.at[at, :], obs_v.at[k, i], os.at[k, i]))
                copies.append(pltpu.make_async_copy(prior.at[:, at], pri_v.at[k, i], ps.at[k, i]))
        return copies

    def proj_load(u):
        k = lax.rem(u, IN)
        return pltpu.make_async_copy(proj.at[:, pl.ds(pl.multiple_of(u * size, size), size)], proj_v.at[k], js.at[k])

    def near_copy(u):
        k, q = lax.rem(u, near_s.shape[0]), lax.rem(u, near_r.shape[0])
        return remote(near_s.at[k], near_r.at[q], ns.at[k], nr.at[q], r, mate)

    def far_copies(u):
        k, q = lax.rem(u, far_s.shape[0]), lax.rem(u, far_r.shape[0])
        return [remote(far_s.at[k, t - 1], far_r.at[q, t - 1], fs.at[k, t - 1], fr.at[q, t - 1], r, other(t, True))
                for t in range(1, chips)]

    def base_copies(u):
        k = lax.rem(u, keep.shape[0])
        return [remote(keep.at[k, t, half:half + sims], out_ref.at[:, span(other(t, True), u)], ts.at[k, t - 1], tr.at[u, t - 1], r, mate)
                for t in range(1, chips)]

    def base_arrivals(u):
        return [remote(keep.at[0, t, half:half + sims], out_ref.at[:, span(other(t, False), u)], ts.at[0, t - 1], tr.at[u, t - 1], r, mate)
                for t in range(1, chips)]

    def own_copy(u, same=True):
        k = lax.rem(u, keep.shape[0])
        return remote(keep.at[k, 0, half:half + sims], out_ref.at[:, span(other(0, same), u)], us.at[k], ur.at[u], r, mate)

    chunks = 8 if units % 8 == 0 else units
    many = units // chunks

    def back_copies(j):
        at = pl.ds(j * many, many)
        return [remote(g_s.at[(t - 1) * 2 + e, at], g_r.at[(t - 1) * 2 + e, at], gs.at[j, (t - 1) * 2 + e], gr.at[j, (t - 1) * 2 + e], r, other(t, e == 0))
                for t in range(1, chips) for e in range(2)]

    for u in range(min(2, units)):
        for cp in loads(u):
            cp.start()
        proj_load(u).start()
    meet([(r, lax.rem(c + d, n_col)) for d in range(1, n_col)]
         + [(beside, c)] + [(lax.rem(high + d, pairs) * 2 + low, c) for d in range(1, pairs)])
    acc[...] = jnp.zeros_like(acc)

    def sum_chip(u):
        near_copy(u).wait_recv()

        @pl.when(u >= far_s.shape[0])
        def _():
            for cp in far_copies(u - far_s.shape[0]):
                cp.wait_send()

        k, q, e = lax.rem(u, far_s.shape[0]), lax.rem(u, near_r.shape[0]), lax.rem(u, keep.shape[0])
        away, base = far_copies(u), base_copies(u)
        for t in list(range(1, chips)) + [0]:
            lo = keep[e, t, :half] + near_r[q, t, half:]
            hi = keep[e, t, half:] + near_r[q, t, :half]
            if t > 0:
                far_s[k, t - 1, :half] = lo.astype(jnp.bfloat16)
                far_s[k, t - 1, half:] = hi.astype(jnp.bfloat16)
                away[t - 1].start()
                out_ref[:, span(other(t, True), u)] = lo[:sims]
                keep[e, t, half:half + sims] = hi[:sims]
                base[t - 1].start()
            else:
                keep[e, 0, :half] = lo
                keep[e, 0, half:] = hi

    def multiply(u):
        n, k, e = lax.rem(u, IN), lax.rem(u, near_s.shape[0]), lax.rem(u, keep.shape[0])
        for cp in loads(u):
            cp.wait()

        @pl.when(u >= near_s.shape[0])
        def _():
            near_copy(u - near_s.shape[0]).wait_send()

        @pl.when(u >= keep.shape[0])
        def _():
            for cp in base_copies(u - keep.shape[0]) + [own_copy(u - keep.shape[0])]:
                cp.wait_send()

        for o in range(2):
            for t in range(chips):
                value = lax.dot_general(p_ref[...], obs_v[n, o * chips + t], NT, preferred_element_type=jnp.float32)
                first = value[:sims] + pri_v[n, o * chips + t]
                if o == 0:
                    near_s[k, t, :sims] = first
                    near_s[k, t, sims:] = value[sims:]
                else:
                    keep[e, t, :sims] = first
                    keep[e, t, sims:] = value[sims:]
            if o == 0:
                near_copy(u).start()

    def project(u):
        for cp in far_copies(u):
            cp.wait_recv()
        q, e, n = lax.rem(u, far_r.shape[0]), lax.rem(u, keep.shape[0]), lax.rem(u, IN)
        weight = apod_ref[pl.ds(c * units + u, 1), :]
        for h in range(2):
            for b in range(chips):
                at = slice((h * chips + b) * sims, (h * chips + b + 1) * sims)
                total, last = keep[e, 0, at], None
                for t in range(1, chips):
                    s = h * chips + (b + t) % chips
                    term = far_r[q, t - 1, s * sims:(s + 1) * sims].astype(jnp.float32)
                    if b > 0 and t == chips - b:
                        last = term
                    else:
                        total = total + term
                if b > 0:
                    g_s[(b - 1) * 2 + h, u] = total.astype(jnp.bfloat16)
                    total = total + last
                elif h == 0:
                    out_ref[:, span(c, u)] = total
                else:
                    keep[e, 0, half:half + sims] = total
                    own_copy(u).start()
                w_v[at] = (weight * total).astype(jnp.bfloat16)
        proj_load(u).wait()
        tile = min(512, prows)
        for j in range(0, prows, tile):
            acc[:, j:j + tile] += lax.dot_general(w_v[...], proj_v[n, j:j + tile, :], NT, preferred_element_type=jnp.float32)

        @pl.when(u + 2 < units)
        def _():
            proj_load(u + 2).start()

    early = max(0, min((units + D2 - D3) // many, chunks - 1))

    def step(g, carry):
        @pl.when(g + 2 < units)
        def _():
            for cp in loads(g + 2):
                cp.start()

        @pl.when((g >= D2) & (g < units + D2))
        def _():
            sum_chip(g - D2)

        @pl.when(g < units)
        def _():
            multiply(g)

        @pl.when(g >= D3)
        def _():
            project(g - D3)

        @pl.when(g == units + D2 - 1)
        def _():
            for j in range(early):
                for cp in back_copies(j):
                    cp.start()

        return carry

    lax.fori_loop(0, units + D3, step, 0)

    hs, pb = sims // 2, prows // n_row
    pieces = [(t, h) for t in reversed(range(chips)) for h in range(2)]

    def swap_copy(i):
        t, h = pieces[i]
        return remote(acc.at[half + t * sims + h * hs:half + t * sims + (h + 1) * hs], swap.at[i], s1.at[i], r1.at[i], r, mate)

    def y_copy(i):
        return remote(fb.at[i, 1 - low], yb.at[i], s2.at[i], r2.at[i], beside, c)

    def z_copies(i):
        return [remote(gb.at[i, lax.rem(high + d, pairs)], zb.at[i, d - 1], s3.at[i, d - 1], r3.at[i, d - 1], lax.rem(high + d, pairs) * 2 + low, c)
                for d in range(1, pairs)]

    def x_copy(i):
        return remote(hb.at[i], xb.at[i], s4.at[i], r4.at[i], r, other(pieces[i][0], True))

    every = range(len(pieces))
    for i in every:
        swap_copy(i).start()
    for i in every:
        t, h = pieces[i]
        swap_copy(i).wait_recv()
        for k in range(n_row):
            fb[i, k % 2, k // 2] = acc[t * sims + h * hs:t * sims + (h + 1) * hs, k * pb:(k + 1) * pb] + swap[i, :, k * pb:(k + 1) * pb]
        y_copy(i).start()
    for i in every:
        y_copy(i).wait_recv()
        gb[i] = fb[i, low] + yb[i]
        for cp in z_copies(i):
            cp.start()
    for i in every:
        total = gb[i, high]
        for d, cp in enumerate(z_copies(i)):
            cp.wait_recv()
            total = total + zb[i, d]
        hb[i] = total
        if pieces[i][0] > 0:
            x_copy(i).start()
    for j in range(early, chunks):
        for cp in back_copies(j):
            cp.start()

    def finish(j):
        for cp in back_copies(j):
            cp.wait_recv()

        def one(u, carry):
            for cp in base_arrivals(u):
                cp.wait_recv()
            own_copy(u, False).wait_recv()
            for t in range(1, chips):
                for e in range(2):
                    at = span(other(chips - t, e == 0), u)
                    out_ref[:, at] = out_ref[:, at] + g_r[(t - 1) * 2 + e, u].astype(jnp.float32)
            return carry

        lax.fori_loop(j * many, (j + 1) * many, one, 0)

    for j in range(chunks - 1):
        finish(j)
    for h in range(2):
        total = hb[pieces.index((0, h))]
        for t in range(1, chips):
            i = pieces.index((t, h))
            x_copy(i).wait_recv()
            total = total + xb[i]
        pout_ref[h * hs:(h + 1) * hs, :] = total
    finish(chunks - 1)

    for i in every:
        swap_copy(i).wait_send()
        y_copy(i).wait_send()
        for cp in z_copies(i):
            cp.wait_send()
        if pieces[i][0] > 0:
            x_copy(i).wait_send()
    for j in range(chunks):
        for cp in back_copies(j):
            cp.wait_send()
    for b in range(min(units, near_s.shape[0])):
        near_copy(units - 1 - b).wait_send()
    for b in range(min(units, far_s.shape[0])):
        for cp in far_copies(units - 1 - b):
            cp.wait_send()
    for b in range(min(units, keep.shape[0])):
        for cp in base_copies(units - 1 - b) + [own_copy(units - 1 - b)]:
            cp.wait_send()


def stream(picked, obs, prior, apod, proj, n_row, n_col):
    depth, (sims, rows), (prows, slab) = obs.shape[1], prior.shape, proj.shape
    size = math.gcd(slab, UNIT)
    units = slab // size
    chips, pairs = n_col // 2, n_row // 2
    all_sims, pb, hs, pieces = n_col * sims, prows // n_row, sims // 2, 2 * chips
    back = 2 * (chips - 1)
    chunks = 8 if units % 8 == 0 else units
    n_keep, n_far = D3 + 2, 2 * (D3 - D2) + 2
    vmem, anywhere = pl.BlockSpec(memory_space=pltpu.VMEM), pl.BlockSpec(memory_space=pl.ANY)
    dma, bf16, f32 = pltpu.SemaphoreType.DMA, jnp.bfloat16, jnp.float32
    return pl.pallas_call(
        functools.partial(stream_kernel, n_row, n_col, units),
        in_specs=[vmem, vmem, anywhere, anywhere, anywhere],
        out_specs=[vmem, vmem],
        out_shape=[jax.ShapeDtypeStruct((sims, rows), f32), jax.ShapeDtypeStruct((sims, pb), f32)],
        scratch_shapes=[
            pltpu.VMEM((IN, n_col, size, depth), bf16),
            pltpu.VMEM((IN, n_col, sims, size), f32),
            pltpu.VMEM((IN, prows, size), bf16),
            pltpu.VMEM((2, chips, all_sims, size), f32),
            pltpu.VMEM((2 * D2, chips, all_sims, size), f32),
            pltpu.VMEM((n_keep, chips, all_sims, size), f32),
            pltpu.VMEM((SENDS, chips - 1, all_sims, size), bf16),
            pltpu.VMEM((n_far, chips - 1, all_sims, size), bf16),
            pltpu.VMEM((all_sims, size), bf16),
            pltpu.VMEM((all_sims, prows), f32),
            pltpu.VMEM((back, units, sims, size), bf16),
            pltpu.VMEM((back, units, sims, size), bf16),
            pltpu.VMEM((pieces, hs, prows), f32),
            pltpu.VMEM((pieces, 2, pairs, hs, pb), f32),
            pltpu.VMEM((pieces, pairs, hs, pb), f32),
            pltpu.VMEM((pieces, pairs, hs, pb), f32),
            pltpu.VMEM((pieces, pairs - 1, hs, pb), f32),
            pltpu.VMEM((pieces, hs, pb), f32),
            pltpu.VMEM((pieces, hs, pb), f32),
            dma((IN, n_col)), dma((IN, n_col)), dma((IN,)), dma((2,)), dma((2 * D2,)),
            dma((SENDS, chips - 1)), dma((n_far, chips - 1)),
            dma((n_keep, chips - 1)), dma((units, chips - 1)), dma((n_keep,)), dma((units,)),
            dma((chunks, back)), dma((chunks, back)),
            dma((pieces,)), dma((pieces,)), dma((pieces,)), dma((pieces,)),
            dma((pieces, pairs - 1)), dma((pieces, pairs - 1)), dma((pieces,)), dma((pieces,)),
        ],
        compiler_params=pltpu.CompilerParams(has_side_effects=True, collective_id=1, vmem_limit_bytes=LIMIT),
        name="stream",
    )(picked, apod.reshape(n_col * units, size), obs, prior, proj)


def on_device(n_row, n_col, obs_panel, skies, panel_index, prior_sum, apod, proj_panel):
    rows_blk, sims = skies.shape
    local_idx = panel_index - lax.axis_index("row") * rows_blk
    inside = (local_idx >= 0) & (local_idx < rows_blk)
    taken = jnp.take(skies, jnp.clip(local_idx, 0, rows_blk - 1), axis=0)
    own = jnp.where(inside[:, None], taken, jnp.zeros((), jnp.bfloat16)).T
    picked = spread(own, n_row, n_col)
    out, projection = stream(picked, obs_panel, prior_sum.T, apod, proj_panel, n_row, n_col)
    return out.T, projection.T


def solution(mesh):
    in_specs = (P("row", "col"), P("row", "col"), P(), P("row", "col"), P("row"), P(None, ("row", "col")))
    out_specs = (P("row", "col"), P("row", "col"))
    body = functools.partial(on_device, mesh.shape["row"], mesh.shape["col"])
    return jax.shard_map(body, mesh=mesh, in_specs=in_specs, out_specs=out_specs, check_vma=False)
```

time: 177 us -> 161 us (0.910)
  Pallas kernels: 151 us -> 135 us
    pallas_call x2 -> x1, Pallas kernels: 132 us -> 116 us  [stream(): pl.pallas_call(functools.partial(stream_kernel, n_row, n_col, units), in_...]
    unnamed x4 -> x3, local copies, waits for them, and re-layouts: 7.22 us -> 13.1 us
    reshape x2 -> x1, local copies, waits for them, and re-layouts: 6.2 us -> 0.92 us  [stream(): apod.reshape(n_col * units, size)]
  transfers between devices with their start and end apart: 1 -> 0, of which waited for: 0 -> 0; matrix products, arithmetic and copies ran while one was open for 3% -> 0% of each run, Pallas kernels for 0% -> 0%
where the time goes in v1:
time: 161 us
  Pallas kernels  135 us (84%)
  local copies, waits for them, and re-layouts  23.4 us (15%)
    pallas_call x1, Pallas kernels, stream(): pl.pallas_call(functools.partial(stream_kernel, n_row, n_col, units), in_...  116 us
    pallas_call x1, Pallas kernels, spread(): pl.pallas_call(functools.partial(spread_kernel, n_row, n_col), out_shape=...  19.3 us
    unnamed x3, local copies, waits for them, and re-layouts  13.1 us
    gather x2, local copies, waits for them, and re-layouts, on_device(): taken = jnp.take(skies, jnp.clip(local_idx, 0, rows_blk - 1), axis=0)  9.38 us

profile of v1, /device:TPU:0, one launch (start us, length us, event | category | flops | bytes accessed | tf_op | source)
XLA Modules:
  0.0 160.7 jit_solution(16538690762655418369)
XLA Ops:
  0.6 0.7 compare_and_fusion.1
  1.3 0.7 fusion
  2.1 0.9 reshape.13.apod_ref
  3.0 6.6 %copy.8 = bf16[24576,64]{1,0:T(8,128)(2,1)} copy(bf16[24576,64]{0,1:T(8,128)(2,1)} %param.7) | data formatting | bytes 6291456 | tf_op args[1]
  9.5 9.2 %gather_fusion = bf16[2048,64]{1,0:T(8,128)(2,1)S(1)} fusion(bf16[24576,64]{1,0:T(8,128)(2,1)} %copy.8, s32[2048]{0:T(1024)S(1)} %fusion), kind=kCustom, calls=%fused_computation | custom fusion | bytes 532480 | tf_op jit(solution)/shard_map/jit(_take)/gather | solution.py:461
  18.7 0.2 copy.9
  19.0 19.3 %spread.1.p_ref = bf16[256,512]{1,0:T(8,128)(2,1)S(1)} custom-call(bf16[64,2048]{1,0:T(8,128)(2,1)S(1)} %select_bitcast_fusion.own_ref), custom_call_target="tpu_custom_call" | custom-call | tf_op jit(solution)/shard_map/spread/pallas_call | solution.py:115
  38.3 115.9 %stream.1 = (f32[64,24576]{1,0:T(8,128)}, f32[64,256]{1,0:T(8,128)S(1)}) custom-call(bf16[256,512]{1,0:T(8,128)(2,1)S(1)} %spread.1.p_ref, f32[96,256]{1,0:T(8,128)S(1)} %reshape.13.apod_ref, bf16[24576,512]{1,0:T(8,128)(2,1)} %obs.1, f32[64,24576]{1,0:T(8,128)} %bitcast.7, bf16[2048,6144]{1,0:T(8,128)(2,1)} %proj.1), custom_call_target="tpu_custom_call" | custom-call | tf_op jit(solution)/shard_map/stream/pallas_call | solution.py:420
  154.1 5.9 %copy.12 = f32[24576,64]{0,1:T(8,128)} copy(f32[24576,64]{0,1:T(8,128)} %bitcast.6) | data formatting | bytes 12582912
  160.1 0.6 copy.13
  (1 shorter events, 0.0 us)

commit v2 on v1

--- a/solution.py
+++ b/solution.py
@@ -13,7 +13,8 @@
 UNIT = 256
 D2, D3 = 1, 4
 IN, SENDS = 3, 3
-LIMIT = 48 * 1024 * 1024
+LIMIT = 46 * 1024 * 1024
+LANES = 128
 
 
 def remote(src, dst, send, recv, row, col):
@@ -22,119 +23,130 @@
     )
 
 
-def meet(devices):
-    barrier = pltpu.get_barrier_semaphore()
-    for device in devices:
-        pl.semaphore_signal(barrier, inc=1, device_id=device, device_id_type=MESH)
-    pl.semaphore_wait(barrier, len(devices))
-
-
-def meet_all(n_row, n_col):
-    barrier = pltpu.get_barrier_semaphore()
-    me = lax.axis_index("row") * n_col + lax.axis_index("col")
-    every = n_row * n_col
+def greet(n_row, n_col):
+    me, every = lax.axis_index("row") * n_col + lax.axis_index("col"), n_row * n_col
 
     def tell(i, carry):
         to = lax.rem(me + i, every)
-        pl.semaphore_signal(barrier, inc=1, device_id=(lax.div(to, n_col), lax.rem(to, n_col)), device_id_type=MESH)
+        pl.semaphore_signal(pltpu.get_barrier_semaphore(), inc=1, device_id=(lax.div(to, n_col), lax.rem(to, n_col)), device_id_type=MESH)
         return carry
 
     lax.fori_loop(1, every, tell, 0)
-    pl.semaphore_wait(barrier, every - 1)
-
-
-def spread_kernel(n_row, n_col, own_ref, out_ref, land, mine, gather, send1, recv1, send2, recv2):
-    r, c = lax.axis_index("row"), lax.axis_index("col")
-    meet_all(n_row, n_col)
-    sims, panel = own_ref.shape
-    part = panel // n_row
-    rep = n_row // n_col
+
+
+def tabulate(r, idx_ref, held, table, where_v, where_s, loads, where_sem):
+    groups, sims, width = held.shape
+    rows, lanes = groups * width, table.shape[1]
+    parts = lanes // sims
+    span = width // parts
+    at = idx_ref[...] - r * rows
+    near = jnp.clip(at, 0, rows - 1)
+    where_v[...] = lax.div(near, width) * span + lax.rem(near, span)
+    codes = pltpu.make_async_copy(where_v, where_s, where_sem)
+    codes.start()
+    one = (lax.broadcasted_iota(jnp.int32, (span, span), 0) == lax.broadcasted_iota(jnp.int32, (span, span), 1)).astype(held.dtype)
+    batch = max(1, groups // 4)
+    for first in range(0, groups, batch):
+        some = range(first, min(groups, first + batch))
+        for g in some:
+            loads[g].wait()
+        for g in some:
+            block = jnp.concatenate([held[g, :, b * span:(b + 1) * span] for b in range(parts)], axis=0)
+            table[g * span:(g + 1) * span, :] = lax.dot_general(one, block, NT, preferred_element_type=jnp.float32)
+    codes.wait()
+    where_v[...] = jnp.where((at >= 0) & (at < rows), lax.rem(lax.div(near, span), parts), -1)
+
+
+def spread(n_row, n_col, r, c, p_ref, table, where_v, where_s, rows_v, own, land, mine, gather, send1, recv1, send2, recv2):
+    halves, sims, part = own.shape[1], own.shape[1] * own.shape[2], own.shape[3]
+    hs, lanes, rep = sims // halves, table.shape[1], n_row // n_col
+    tiles = part // LANES
+    turn = (lax.broadcasted_iota(jnp.int32, (lanes, lanes), 0) == lax.broadcasted_iota(jnp.int32, (lanes, lanes), 1)).astype(own.dtype)
 
     def part_of(row):
         return lax.rem(row, 2) * (n_row // 2) + lax.div(row, 2)
 
-    first = []
-    for d in range(1, n_row):
+    def first_copy(d, h):
         to = lax.rem(r + d, n_row)
-        cp = remote(own_ref.at[:, pl.ds(pl.multiple_of(part_of(to) * part, part), part)], land.at[d - 1],
-                    send1.at[d - 1], recv1.at[d - 1], to, c)
-        cp.start()
-        first.append(cp)
-    total = own_ref[:, pl.ds(pl.multiple_of(part_of(r) * part, part), part)].astype(jnp.float32)
-    for d in range(1, n_row):
-        first[d - 1].wait_recv()
-        total = total + land[d - 1].astype(jnp.float32)
-    mine[...] = total.astype(mine.dtype)
-    sub = lax.rem(part_of(r), rep)
-    col_to = lax.div(part_of(r), rep)
+        return remote(own.at[part_of(to), h], land.at[h, d - 1], send1.at[h, d - 1], recv1.at[h, d - 1], to, c)
+
+    def collect(i, carry):
+        d = lax.rem(i + 1, n_row)
+        k = part_of(lax.rem(r + d, n_row))
+        for t in range(tiles):
+            for j in range(LANES):
+                rows_v[t * LANES + j:t * LANES + j + 1, :] = table[pl.ds(where_s[k * tiles + t, j], 1), :]
+        for t in range(tiles):
+            flat = lax.dot_general(turn, rows_v[t * LANES:(t + 1) * LANES, :].astype(own.dtype), NT, preferred_element_type=jnp.float32)
+            which = where_v[pl.ds(k * tiles + t, 1), :]
+            total = jnp.zeros((sims, LANES), jnp.float32)
+            for b in range(lanes // sims):
+                total = jnp.where(which == b, flat[b * sims:(b + 1) * sims], total)
+            for h in range(halves):
+                own[k, h, :, t * LANES:(t + 1) * LANES] = total[h * hs:(h + 1) * hs].astype(own.dtype)
+
+        @pl.when(d > 0)
+        def _():
+            for h in range(halves):
+                first_copy(d, h).start()
+
+        return carry
+
+    lax.fori_loop(0, n_row, collect, 0)
+    sub, col_to = lax.rem(part_of(r), rep), lax.div(part_of(r), rep)
     slot = sub * n_col + c
-    second = []
-    for d in range(n_row):
-        to = lax.rem(r + d, n_row)
-        cp = remote(mine, gather.at[slot], send2.at[d], recv2.at[slot], to, col_to)
-        second.append(cp)
-        if d > 0:
-            cp.start()
-        else:
+
+    def second_copy(d, h):
+        return remote(mine.at[h], gather.at[slot, h], send2.at[h, d], recv2.at[h, slot], lax.rem(r + d, n_row), col_to)
+
+    for h in range(halves):
+        total = own[part_of(r), h].astype(jnp.float32)
+        for d in range(1, n_row):
+            first_copy(d, h).wait_recv()
+            total = total + land[h, d - 1].astype(jnp.float32)
+        mine[h] = total.astype(mine.dtype)
+        for d in range(1, n_row):
+            second_copy(d, h).start()
+
+        @pl.when(col_to != c)
+        def _():
+            second_copy(0, h).start()
+
+        @pl.when(col_to == c)
+        def _():
+            gather[slot, h] = mine[h]
+
+    chips = n_col // 2
+    core, chip = lax.rem(c, 2), lax.div(c, 2)
+    for h in range(halves):
+        for s in range(rep):
+            for j in range(n_col):
+                @pl.when(jnp.logical_not((c * rep + s == part_of(r)) & (c == j)))
+                def _():
+                    remote(mine.at[h], gather.at[s * n_col + j, h], send2.at[h, 0], recv2.at[h, s * n_col + j], r, c).wait_recv()
+        for q in range(n_col):
+            source = lax.rem(chip + q % chips, chips) * 2 + (core if q // chips == 0 else 1 - core)
+            for s in range(rep):
+                p_ref[q * sims + h * hs:q * sims + (h + 1) * hs, s * part:(s + 1) * part] = gather[s * n_col + source, h]
+
+    def drain():
+        for h in range(halves):
+            for d in range(1, n_row):
+                first_copy(d, h).wait_send()
+                second_copy(d, h).wait_send()
+
             @pl.when(col_to != c)
             def _():
-                cp.start()
-
-            @pl.when(col_to == c)
-            def _():
-                gather[slot] = mine[...]
-    for s in range(rep):
-        for j in range(n_col):
-            here = (c * rep + s == part_of(r)) & (c == j)
-
-            @pl.when(jnp.logical_not(here))
-            def _():
-                remote(mine, gather.at[s * n_col + j], send2.at[0], recv2.at[s * n_col + j], r, c).wait_recv()
-    chips = n_col // 2
-    core, chip = lax.rem(c, 2), lax.div(c, 2)
-    for q in range(n_col):
-        other, shift = q // chips, q % chips
-        source = lax.rem(chip + shift, chips) * 2 + (core if other == 0 else 1 - core)
-        for s in range(rep):
-            out_ref[q * sims:(q + 1) * sims, s * part:(s + 1) * part] = gather[s * n_col + source]
-    for cp in first:
-        cp.wait_send()
-    for d in range(n_row):
-        if d > 0:
-            second[d].wait_send()
-        else:
-            @pl.when(col_to != c)
-            def _():
-                second[0].wait_send()
-
-
-def spread(own, n_row, n_col):
-    sims, panel = own.shape
-    part = panel // n_row
-    vmem = pl.BlockSpec(memory_space=pltpu.VMEM)
-    return pl.pallas_call(
-        functools.partial(spread_kernel, n_row, n_col),
-        out_shape=jax.ShapeDtypeStruct((sims * n_col, panel // n_col), own.dtype),
-        in_specs=[vmem],
-        out_specs=vmem,
-        scratch_shapes=[
-            pltpu.VMEM((n_row - 1, sims, part), own.dtype),
-            pltpu.VMEM((sims, part), own.dtype),
-            pltpu.VMEM((n_row, sims, part), own.dtype),
-            pltpu.SemaphoreType.DMA((n_row - 1,)),
-            pltpu.SemaphoreType.DMA((n_row - 1,)),
-            pltpu.SemaphoreType.DMA((n_row,)),
-            pltpu.SemaphoreType.DMA((n_row,)),
-        ],
-        compiler_params=pltpu.CompilerParams(has_side_effects=True, collective_id=0, vmem_limit_bytes=LIMIT),
-        name="spread",
-    )(own)
-
-
-def stream_kernel(n_row, n_col, units, p_ref, apod_ref, obs, prior, proj, out_ref, pout_ref,
-                  obs_v, pri_v, proj_v, near_s, near_r, keep, far_s, far_r, w_v, acc, g_s, g_r,
+                second_copy(0, h).wait_send()
+
+    return drain
+
+
+def stream_kernel(n_row, n_col, units, idx_ref, maps, apod, obs, prior, proj, out_ref, pout_ref,
+                  held, table, where_v, where_s, rows_v, own, land, mine, gather, p_ref,
+                  apod_ref, obs_v, pri_v, proj_v, near_s, near_r, keep, far_s, far_r, w_v, acc, g_s, g_r,
                   swap, fb, yb, gb, zb, hb, xb,
-                  os, ps, js, ns, nr, fs, fr, ts, tr, us, ur, gs, gr, s1, r1, s2, r2, s3, r3, s4, r4):
+                  ms, ws, s5, r5, s6, r6, aps, os, ps, js, ns, nr, fs, fr, ts, tr, us, ur, gs, gr, s1, r1, s2, r2, s3, r3, s4, r4):
     r, c = lax.axis_index("row"), lax.axis_index("col")
     chips, pairs = n_col // 2, n_row // 2
     core, chip = lax.rem(c, 2), lax.div(c, 2)
@@ -193,13 +205,21 @@
         return [remote(g_s.at[(t - 1) * 2 + e, at], g_r.at[(t - 1) * 2 + e, at], gs.at[j, (t - 1) * 2 + e], gr.at[j, (t - 1) * 2 + e], r, other(t, e == 0))
                 for t in range(1, chips) for e in range(2)]
 
+    width = held.shape[2]
+    tables = [pltpu.make_async_copy(maps.at[:, g * width:(g + 1) * width], held.at[g], ms.at[g]) for g in range(held.shape[0])]
+    weights = pltpu.make_async_copy(apod, apod_ref, aps)
+    for cp in tables + [weights]:
+        cp.start()
     for u in range(min(2, units)):
         for cp in loads(u):
             cp.start()
         proj_load(u).start()
-    meet([(r, lax.rem(c + d, n_col)) for d in range(1, n_col)]
-         + [(beside, c)] + [(lax.rem(high + d, pairs) * 2 + low, c) for d in range(1, pairs)])
+    greet(n_row, n_col)
     acc[...] = jnp.zeros_like(acc)
+    tabulate(r, idx_ref, held, table, where_v, where_s, tables, ws)
+    pl.semaphore_wait(pltpu.get_barrier_semaphore(), n_row * n_col - 1)
+    drain = spread(n_row, n_col, r, c, p_ref, table, where_v, where_s, rows_v, own, land, mine, gather, s5, r5, s6, r6)
+    weights.wait()
 
     def sum_chip(u):
         near_copy(u).wait_recv()
@@ -256,7 +276,8 @@
         for cp in far_copies(u):
             cp.wait_recv()
         q, e, n = lax.rem(u, far_r.shape[0]), lax.rem(u, keep.shape[0]), lax.rem(u, IN)
-        weight = apod_ref[pl.ds(c * units + u, 1), :]
+        wide = size // LANES
+        weight = jnp.concatenate([apod_ref[pl.ds((c * units + u) * wide + i, 1), :] for i in range(wide)], axis=1)
         for h in range(2):
             for b in range(chips):
                 at = slice((h * chips + b) * sims, (h * chips + b + 1) * sims)
@@ -386,6 +407,7 @@
         pout_ref[h * hs:(h + 1) * hs, :] = total
     finish(chunks - 1)
 
+    drain()
     for i in every:
         swap_copy(i).wait_send()
         y_copy(i).wait_send()
@@ -406,8 +428,12 @@
             cp.wait_send()
 
 
-def stream(picked, obs, prior, apod, proj, n_row, n_col):
+def stream(index, maps, obs, prior, apod, proj, n_row, n_col):
     depth, (sims, rows), (prows, slab) = obs.shape[1], prior.shape, proj.shape
+    panel, part = index.shape[0], index.shape[0] // n_row
+    parts = max(1, LANES // sims)
+    width = parts * math.gcd(UNIT, rows // parts)
+    halves = 2
     size = math.gcd(slab, UNIT)
     units = slab // size
     chips, pairs = n_col // 2, n_row // 2
@@ -415,14 +441,25 @@
     back = 2 * (chips - 1)
     chunks = 8 if units % 8 == 0 else units
     n_keep, n_far = D3 + 2, 2 * (D3 - D2) + 2
-    vmem, anywhere = pl.BlockSpec(memory_space=pltpu.VMEM), pl.BlockSpec(memory_space=pl.ANY)
+    vmem, anywhere = pl.BlockSpec(memory_space=pltpu.VMEM), pl.BlockSpec(memory_space=pltpu.HBM)
     dma, bf16, f32 = pltpu.SemaphoreType.DMA, jnp.bfloat16, jnp.float32
     return pl.pallas_call(
         functools.partial(stream_kernel, n_row, n_col, units),
-        in_specs=[vmem, vmem, anywhere, anywhere, anywhere],
+        in_specs=[vmem] + [anywhere] * 5,
         out_specs=[vmem, vmem],
         out_shape=[jax.ShapeDtypeStruct((sims, rows), f32), jax.ShapeDtypeStruct((sims, pb), f32)],
         scratch_shapes=[
+            pltpu.VMEM((rows // width, sims, width), bf16),
+            pltpu.VMEM((rows // parts, parts * sims), f32),
+            pltpu.VMEM((panel // LANES, LANES), jnp.int32),
+            pltpu.SMEM((panel // LANES, LANES), jnp.int32),
+            pltpu.VMEM((part, parts * sims), f32),
+            pltpu.VMEM((n_row, halves, sims // halves, part), bf16),
+            pltpu.VMEM((halves, n_row - 1, sims // halves, part), bf16),
+            pltpu.VMEM((halves, sims // halves, part), bf16),
+            pltpu.VMEM((n_row, halves, sims // halves, part), bf16),
+            pltpu.VMEM((all_sims, depth), bf16),
+            pltpu.VMEM((rows // LANES, LANES), f32),
             pltpu.VMEM((IN, n_col, size, depth), bf16),
             pltpu.VMEM((IN, n_col, sims, size), f32),
             pltpu.VMEM((IN, prows, size), bf16),
@@ -442,26 +479,21 @@
             pltpu.VMEM((pieces, pairs - 1, hs, pb), f32),
             pltpu.VMEM((pieces, hs, pb), f32),
             pltpu.VMEM((pieces, hs, pb), f32),
-            dma((IN, n_col)), dma((IN, n_col)), dma((IN,)), dma((2,)), dma((2 * D2,)),
+            dma((rows // width,)), dma, dma((halves, n_row - 1)), dma((halves, n_row - 1)), dma((halves, n_row)), dma((halves, n_row)),
+            dma, dma((IN, n_col)), dma((IN, n_col)), dma((IN,)), dma((2,)), dma((2 * D2,)),
             dma((SENDS, chips - 1)), dma((n_far, chips - 1)),
             dma((n_keep, chips - 1)), dma((units, chips - 1)), dma((n_keep,)), dma((units,)),
             dma((chunks, back)), dma((chunks, back)),
             dma((pieces,)), dma((pieces,)), dma((pieces,)), dma((pieces,)),
             dma((pieces, pairs - 1)), dma((pieces, pairs - 1)), dma((pieces,)), dma((pieces,)),
         ],
-        compiler_params=pltpu.CompilerParams(has_side_effects=True, collective_id=1, vmem_limit_bytes=LIMIT),
+        compiler_params=pltpu.CompilerParams(has_side_effects=True, collective_id=0, vmem_limit_bytes=LIMIT),
         name="stream",
-    )(picked, apod.reshape(n_col * units, size), obs, prior, proj)
+    )(index.reshape(panel // LANES, LANES), *[pltpu.with_memory_space_constraint(x, pltpu.HBM) for x in (maps, apod.reshape(rows // LANES, LANES), obs, prior, proj)])
 
 
 def on_device(n_row, n_col, obs_panel, skies, panel_index, prior_sum, apod, proj_panel):
-    rows_blk, sims = skies.shape
-    local_idx = panel_index - lax.axis_index("row") * rows_blk
-    inside = (local_idx >= 0) & (local_idx < rows_blk)
-    taken = jnp.take(skies, jnp.clip(local_idx, 0, rows_blk - 1), axis=0)
-    own = jnp.where(inside[:, None], taken, jnp.zeros((), jnp.bfloat16)).T
-    picked = spread(own, n_row, n_col)
-    out, projection = stream(picked, obs_panel, prior_sum.T, apod, proj_panel, n_row, n_col)
+    out, projection = stream(panel_index, skies.T, obs_panel, prior_sum.T, apod, proj_panel, n_row, n_col)
     return out.T, projection.T
 
 

time: 161 us -> 136 us (0.84)
  local copies, waits for them, and re-layouts: 23.4 us -> 4.02 us
  Pallas kernels: 135 us -> 131 us
    pallas_call x1 -> x0, Pallas kernels: 19.3 us -> none  [spread(): pl.pallas_call(functools.partial(spread_kernel, n_row, n_col), out_shape=...]
    pallas_call x1, Pallas kernels: 116 us -> 131 us  [stream(): pl.pallas_call(functools.partial(stream_kernel, n_row, n_col, units), in_...]
    gather x2 -> x0, local copies, waits for them, and re-layouts: 9.38 us -> none  [on_device(): taken = jnp.take(skies, jnp.clip(local_idx, 0, rows_blk - 1), axis=0)]
    unnamed x3 -> x4, local copies, waits for them, and re-layouts: 13.1 us -> 4.02 us
where the time goes in v2:
time: 136 us
  Pallas kernels  131 us (96%)
  local copies, waits for them, and re-layouts  4.02 us (3%)
    pallas_call x1, Pallas kernels, stream(): pl.pallas_call(functools.partial(stream_kernel, n_row, n_col, units), in_...  131 us
    unnamed x4, local copies, waits for them, and re-layouts  4.02 us

profile of v2, /device:TPU:0, one launch (start us, length us, event | category | flops | bytes accessed | tf_op | source)
XLA Modules:
  0.0 135.7 jit_solution(16752903121933149791)
XLA Ops:
  0.6 0.0 copy-start
  0.6 0.7 copy-done
  1.3 131.0 %stream.1 = (f32[64,24576]{1,0:T(8,128)S(1)}, f32[64,256]{1,0:T(8,128)S(1)}) custom-call(s32[16,128]{1,0:T(8,128)S(1)} %bitcast.8, bf16[64,24576]{1,0:T(8,128)(2,1)} %bitcast.10, f32[192,128]{1,0:T(8,128)} %bitcast.11, bf16[24576,512]{1,0:T(8,128)(2,1)} %obs.1, f32[64,24576]{1,0:T(8,128)} %bitcast.9, bf16[2048,6144]{1,0:T(8,128)(2,1)} %proj.1), custom_call_target="tpu_custom_call" | custom-call | tf_op jit(solution)/shard_map/stream/pallas_call | solution.py:446
  132.3 2.7 %copy.10 = f32[24576,64]{0,1:T(8,128)} copy(f32[24576,64]{0,1:T(8,128)S(1)} %bitcast.6) | data formatting | bytes 12582912
  135.0 0.6 copy.11
Async XLA Ops:
  0.6 0.7 copy-start

commit v3 on v2

--- a/solution.py
+++ b/solution.py
@@ -15,6 +15,7 @@
 IN, SENDS = 3, 3
 LIMIT = 46 * 1024 * 1024
 LANES = 128
+AHEAD = 3
 
 
 def remote(src, dst, send, recv, row, col):
@@ -23,15 +24,9 @@
     )
 
 
-def greet(n_row, n_col):
-    me, every = lax.axis_index("row") * n_col + lax.axis_index("col"), n_row * n_col
-
-    def tell(i, carry):
-        to = lax.rem(me + i, every)
-        pl.semaphore_signal(pltpu.get_barrier_semaphore(), inc=1, device_id=(lax.div(to, n_col), lax.rem(to, n_col)), device_id_type=MESH)
-        return carry
-
-    lax.fori_loop(1, every, tell, 0)
+def greet(devices):
+    for device in devices:
+        pl.semaphore_signal(pltpu.get_barrier_semaphore(), inc=1, device_id=device, device_id_type=MESH)
 
 
 def tabulate(r, idx_ref, held, table, where_v, where_s, loads, where_sem):
@@ -45,19 +40,22 @@
     codes = pltpu.make_async_copy(where_v, where_s, where_sem)
     codes.start()
     one = (lax.broadcasted_iota(jnp.int32, (span, span), 0) == lax.broadcasted_iota(jnp.int32, (span, span), 1)).astype(held.dtype)
-    batch = max(1, groups // 4)
+    pair = 2 if groups % 2 == 0 else 1
+    batch = max(1, groups // pair // 4) * pair
     for first in range(0, groups, batch):
         some = range(first, min(groups, first + batch))
         for g in some:
             loads[g].wait()
-        for g in some:
-            block = jnp.concatenate([held[g, :, b * span:(b + 1) * span] for b in range(parts)], axis=0)
-            table[g * span:(g + 1) * span, :] = lax.dot_general(one, block, NT, preferred_element_type=jnp.float32)
+        for g in some[::pair]:
+            block = jnp.concatenate([held[i, :, b * span:(b + 1) * span] for i in range(g, g + pair) for b in range(parts)], axis=0)
+            turned = lax.dot_general(one, block, NT, preferred_element_type=jnp.float32)
+            for i in range(pair):
+                table[(g + i) * span:(g + i + 1) * span, :] = turned[:, i * lanes:(i + 1) * lanes]
     codes.wait()
     where_v[...] = jnp.where((at >= 0) & (at < rows), lax.rem(lax.div(near, span), parts), -1)
 
 
-def spread(n_row, n_col, r, c, p_ref, table, where_v, where_s, rows_v, own, land, mine, gather, send1, recv1, send2, recv2):
+def spread(n_row, n_col, r, c, peers, ready, p_ref, table, where_v, where_s, rows_v, own, land, mine, gather, send1, recv1, send2, recv2):
     halves, sims, part = own.shape[1], own.shape[1] * own.shape[2], own.shape[3]
     hs, lanes, rep = sims // halves, table.shape[1], n_row // n_col
     tiles = part // LANES
@@ -85,6 +83,11 @@
             for h in range(halves):
                 own[k, h, :, t * LANES:(t + 1) * LANES] = total[h * hs:(h + 1) * hs].astype(own.dtype)
 
+        return d
+
+    def collect_and_send(i, carry):
+        d = collect(i, carry)
+
         @pl.when(d > 0)
         def _():
             for h in range(halves):
@@ -92,7 +95,16 @@
 
         return carry
 
-    lax.fori_loop(0, n_row, collect, 0)
+    ahead = min(AHEAD, n_row - 1)
+    lax.fori_loop(0, ahead, lambda i, carry: (collect(i, carry), carry)[1], 0)
+    pl.semaphore_wait(pltpu.get_barrier_semaphore(), n_row + n_col - 2)
+    for device in peers:
+        pl.semaphore_signal(ready, inc=1, device_id=device, device_id_type=MESH)
+    for d in range(1, ahead + 1):
+        for h in range(halves):
+            first_copy(d, h).start()
+    lax.fori_loop(ahead, n_row, collect_and_send, 0)
+    pl.semaphore_wait(ready, n_col - 1)
     sub, col_to = lax.rem(part_of(r), rep), lax.div(part_of(r), rep)
     slot = sub * n_col + c
 
@@ -146,7 +158,7 @@
                   held, table, where_v, where_s, rows_v, own, land, mine, gather, p_ref,
                   apod_ref, obs_v, pri_v, proj_v, near_s, near_r, keep, far_s, far_r, w_v, acc, g_s, g_r,
                   swap, fb, yb, gb, zb, hb, xb,
-                  ms, ws, s5, r5, s6, r6, aps, os, ps, js, ns, nr, fs, fr, ts, tr, us, ur, gs, gr, s1, r1, s2, r2, s3, r3, s4, r4):
+                  ready, ms, ws, s5, r5, s6, r6, aps, os, ps, js, ns, nr, fs, fr, ts, tr, us, ur, gs, gr, s1, r1, s2, r2, s3, r3, s4, r4):
     r, c = lax.axis_index("row"), lax.axis_index("col")
     chips, pairs = n_col // 2, n_row // 2
     core, chip = lax.rem(c, 2), lax.div(c, 2)
@@ -208,17 +220,15 @@
     width = held.shape[2]
     tables = [pltpu.make_async_copy(maps.at[:, g * width:(g + 1) * width], held.at[g], ms.at[g]) for g in range(held.shape[0])]
     weights = pltpu.make_async_copy(apod, apod_ref, aps)
-    for cp in tables + [weights]:
+    for cp in tables:
         cp.start()
-    for u in range(min(2, units)):
-        for cp in loads(u):
-            cp.start()
-        proj_load(u).start()
-    greet(n_row, n_col)
+    line, peers = [(lax.rem(r + d, n_row), c) for d in range(1, n_row)], [(r, lax.rem(c + d, n_col)) for d in range(1, n_col)]
+    greet(line + peers)
     acc[...] = jnp.zeros_like(acc)
     tabulate(r, idx_ref, held, table, where_v, where_s, tables, ws)
-    pl.semaphore_wait(pltpu.get_barrier_semaphore(), n_row * n_col - 1)
-    drain = spread(n_row, n_col, r, c, p_ref, table, where_v, where_s, rows_v, own, land, mine, gather, s5, r5, s6, r6)
+    for cp in [weights] + [cp for u in range(min(2, units)) for cp in loads(u) + [proj_load(u)]]:
+        cp.start()
+    drain = spread(n_row, n_col, r, c, peers, ready, p_ref, table, where_v, where_s, rows_v, own, land, mine, gather, s5, r5, s6, r6)
     weights.wait()
 
     def sum_chip(u):
@@ -479,7 +489,7 @@
             pltpu.VMEM((pieces, pairs - 1, hs, pb), f32),
             pltpu.VMEM((pieces, hs, pb), f32),
             pltpu.VMEM((pieces, hs, pb), f32),
-            dma((rows // width,)), dma, dma((halves, n_row - 1)), dma((halves, n_row - 1)), dma((halves, n_row)), dma((halves, n_row)),
+            pltpu.SemaphoreType.REGULAR, dma((rows // width,)), dma, dma((halves, n_row - 1)), dma((halves, n_row - 1)), dma((halves, n_row)), dma((halves, n_row)),
             dma, dma((IN, n_col)), dma((IN, n_col)), dma((IN,)), dma((2,)), dma((2 * D2,)),
             dma((SENDS, chips - 1)), dma((n_far, chips - 1)),
             dma((n_keep, chips - 1)), dma((units, chips - 1)), dma((n_keep,)), dma((units,)),
@@ -492,8 +502,32 @@
     )(index.reshape(panel // LANES, LANES), *[pltpu.with_memory_space_constraint(x, pltpu.HBM) for x in (maps, apod.reshape(rows // LANES, LANES), obs, prior, proj)])
 
 
+def emit_kernel(out_ref, pout_ref, out, pout, sem):
+    rows = math.gcd(out_ref.shape[0], 8)
+    copies = [pltpu.make_async_copy(pout_ref, pout, sem.at[0])]
+    for i in range(out_ref.shape[0] // rows):
+        copies.append(pltpu.make_async_copy(out_ref.at[i * rows:(i + 1) * rows], out.at[i * rows:(i + 1) * rows], sem.at[i + 1]))
+    for cp in copies:
+        cp.start()
+    for cp in copies:
+        cp.wait()
+
+
+def emit(out, pout):
+    vmem, hbm = pl.BlockSpec(memory_space=pltpu.VMEM), pl.BlockSpec(memory_space=pltpu.HBM)
+    return pl.pallas_call(
+        emit_kernel,
+        out_shape=[jax.ShapeDtypeStruct(x.shape, x.dtype) for x in (out, pout)],
+        in_specs=[vmem] * 2,
+        out_specs=[hbm] * 2,
+        scratch_shapes=[pltpu.SemaphoreType.DMA((out.shape[0] // math.gcd(out.shape[0], 8) + 1,))],
+        compiler_params=pltpu.CompilerParams(vmem_limit_bytes=8 * 1024 * 1024),
+        name="emit",
+    )(out, pout)
+
+
 def on_device(n_row, n_col, obs_panel, skies, panel_index, prior_sum, apod, proj_panel):
-    out, projection = stream(panel_index, skies.T, obs_panel, prior_sum.T, apod, proj_panel, n_row, n_col)
+    out, projection = emit(*stream(panel_index, skies.T, obs_panel, prior_sum.T, apod, proj_panel, n_row, n_col))
     return out.T, projection.T
 
 

time: 136 us -> 134 us (0.985)
  local copies, waits for them, and re-layouts: 4.02 us -> 0.69 us
  Pallas kernels: 131 us -> 133 us
    unnamed x4 -> x2, local copies, waits for them, and re-layouts: 4.02 us -> 0.69 us
    pallas_call x0 -> x1, Pallas kernels: none -> 2.77 us  [emit(): pl.pallas_call(emit_kernel, out_shape=[jax.ShapeDtypeStruct(x.shape, x.dt...]
where the time goes in v3:
time: 134 us
  Pallas kernels  133 us (99%)
    pallas_call x1, Pallas kernels, stream(): pl.pallas_call(functools.partial(stream_kernel, n_row, n_col, units), in_...  130 us
    pallas_call x1, Pallas kernels, emit(): pl.pallas_call(emit_kernel, out_shape=[jax.ShapeDtypeStruct(x.shape, x.dt...  2.77 us

profile of v3, /device:TPU:0, one launch (start us, length us, event | category | flops | bytes accessed | tf_op | source)
XLA Modules:
  0.0 133.9 jit_solution(1119014411450789541)
XLA Ops:
  0.6 0.0 copy-start
  0.6 0.7 copy-done
  1.3 129.8 %stream.1 = (f32[64,24576]{1,0:T(8,128)S(1)}, f32[64,256]{1,0:T(8,128)S(1)}) custom-call(s32[16,128]{1,0:T(8,128)S(1)} %bitcast.6, bf16[64,24576]{1,0:T(8,128)(2,1)} %bitcast.8, f32[192,128]{1,0:T(8,128)} %bitcast.9, bf16[24576,512]{1,0:T(8,128)(2,1)} %obs.1, f32[64,24576]{1,0:T(8,128)} %bitcast.7, bf16[2048,6144]{1,0:T(8,128)(2,1)} %proj.1), custom_call_target="tpu_custom_call" | custom-call | tf_op jit(solution)/shard_map/stream/pallas_call | solution.py:456
  131.1 2.8 %emit.1 = (f32[64,24576]{1,0:T(8,128)}, f32[64,256]{1,0:T(8,128)}) custom-call(f32[64,24576]{1,0:T(8,128)S(1)} %get-tuple-element.6.out_ref, f32[64,256]{1,0:T(8,128)S(1)} %get-tuple-element.7.pout_ref), custom_call_target="tpu_custom_call" | custom-call | tf_op jit(solution)/shard_map/emit/pallas_call | solution.py:518
Async XLA Ops:
  0.6 0.7 copy-start

commit v4 on v3

--- a/solution.py
+++ b/solution.py
@@ -12,7 +12,7 @@
 NT = (((1,), (1,)), ((), ()))
 UNIT = 256
 D2, D3 = 1, 4
-IN, SENDS = 3, 3
+SENDS, EARLY = 3, 2
 LIMIT = 46 * 1024 * 1024
 LANES = 128
 AHEAD = 3
@@ -90,8 +90,7 @@
 
         @pl.when(d > 0)
         def _():
-            for h in range(halves):
-                first_copy(d, h).start()
+            first_copy(d, 0).start()
 
         return carry
 
@@ -101,9 +100,11 @@
     for device in peers:
         pl.semaphore_signal(ready, inc=1, device_id=device, device_id_type=MESH)
     for d in range(1, ahead + 1):
-        for h in range(halves):
+        first_copy(d, 0).start()
+    lax.fori_loop(ahead, n_row, collect_and_send, 0)
+    for h in range(1, halves):
+        for d in range(1, n_row):
             first_copy(d, h).start()
-    lax.fori_loop(ahead, n_row, collect_and_send, 0)
     pl.semaphore_wait(ready, n_col - 1)
     sub, col_to = lax.rem(part_of(r), rep), lax.div(part_of(r), rep)
     slot = sub * n_col + c
@@ -130,7 +131,8 @@
 
     chips = n_col // 2
     core, chip = lax.rem(c, 2), lax.div(c, 2)
-    for h in range(halves):
+
+    def arrive(h):
         for s in range(rep):
             for j in range(n_col):
                 @pl.when(jnp.logical_not((c * rep + s == part_of(r)) & (c == j)))
@@ -138,8 +140,9 @@
                     remote(mine.at[h], gather.at[s * n_col + j, h], send2.at[h, 0], recv2.at[h, s * n_col + j], r, c).wait_recv()
         for q in range(n_col):
             source = lax.rem(chip + q % chips, chips) * 2 + (core if q // chips == 0 else 1 - core)
+            at = (h * n_col + q) * hs
             for s in range(rep):
-                p_ref[q * sims + h * hs:q * sims + (h + 1) * hs, s * part:(s + 1) * part] = gather[s * n_col + source, h]
+                p_ref[at:at + hs, s * part:(s + 1) * part] = gather[s * n_col + source, h]
 
     def drain():
         for h in range(halves):
@@ -151,14 +154,14 @@
             def _():
                 second_copy(0, h).wait_send()
 
-    return drain
+    return arrive, drain
 
 
 def stream_kernel(n_row, n_col, units, idx_ref, maps, apod, obs, prior, proj, out_ref, pout_ref,
                   held, table, where_v, where_s, rows_v, own, land, mine, gather, p_ref,
-                  apod_ref, obs_v, pri_v, proj_v, near_s, near_r, keep, far_s, far_r, w_v, acc, g_s, g_r,
+                  apod_ref, obs_v, pri_v, proj_v, near_s, near_r, keep, base_s, own_s, far_s, far_r, w_v, acc, g_s, g_r,
                   swap, fb, yb, gb, zb, hb, xb,
-                  ready, ms, ws, s5, r5, s6, r6, aps, os, ps, js, ns, nr, fs, fr, ts, tr, us, ur, gs, gr, s1, r1, s2, r2, s3, r3, s4, r4):
+                  ready, ms, ws, s5, r5, s6, r6, aps, os, ps, js, ns, nr, es, er, fs, fr, ds, dr, ts, tr, us, ur, gs, gr, s1, r1, s2, r2, s3, r3, s4, r4):
     r, c = lax.axis_index("row"), lax.axis_index("col")
     chips, pairs = n_col // 2, n_row // 2
     core, chip = lax.rem(c, 2), lax.div(c, 2)
@@ -166,7 +169,10 @@
     mate, beside = chip * 2 + 1 - core, high * 2 + 1 - low
     sims, rows = out_ref.shape
     prows, slab = proj.shape
-    size, half = slab // units, chips * sims
+    size, hs = slab // units, sims // 2
+    half, quad = n_col * hs, chips * hs
+    start, keeps = min(EARLY, units // 4), keep.shape[0]
+    hold, lent, stock = near_s.shape[0], far_s.shape[0], obs_v.shape[0]
 
     def other(t, same):
         return lax.rem(chip + t, chips) * 2 + (core if same else 1 - core)
@@ -175,7 +181,7 @@
         return pl.ds(pl.multiple_of(q * slab + u * size, size), size)
 
     def loads(u):
-        k, copies = lax.rem(u, IN), []
+        k, copies = lax.rem(u, stock), []
         for o in range(2):
             for t in range(chips):
                 i, at = o * chips + t, span(other(t, o == 1), u)
@@ -184,7 +190,7 @@
         return copies
 
     def proj_load(u):
-        k = lax.rem(u, IN)
+        k = lax.rem(u, proj_v.shape[0])
         return pltpu.make_async_copy(proj.at[:, pl.ds(pl.multiple_of(u * size, size), size)], proj_v.at[k], js.at[k])
 
     def near_copy(u):
@@ -196,18 +202,27 @@
         return [remote(far_s.at[k, t - 1], far_r.at[q, t - 1], fs.at[k, t - 1], fr.at[q, t - 1], r, other(t, True))
                 for t in range(1, chips)]
 
+    def near_half(u, h):
+        k, q, at = lax.rem(u, hold), lax.rem(u, near_r.shape[0]), slice(h * half, (h + 1) * half)
+        return remote(near_s.at[k, :, at], near_r.at[q, :, at], es.at[u, h], er.at[u, h], r, mate)
+
+    def far_half(u, h):
+        k, q, at = lax.rem(u, lent), lax.rem(u, far_r.shape[0]), slice(h * half, (h + 1) * half)
+        return [remote(far_s.at[k, t - 1, at], far_r.at[q, t - 1, at], ds.at[u, h, t - 1], dr.at[u, h, t - 1], r, other(t, True))
+                for t in range(1, chips)]
+
     def base_copies(u):
-        k = lax.rem(u, keep.shape[0])
-        return [remote(keep.at[k, t, half:half + sims], out_ref.at[:, span(other(t, True), u)], ts.at[k, t - 1], tr.at[u, t - 1], r, mate)
+        k = lax.rem(u, keeps)
+        return [remote(base_s.at[k, t - 1], out_ref.at[:, span(other(t, True), u)], ts.at[k, t - 1], tr.at[u, t - 1], r, mate)
                 for t in range(1, chips)]
 
     def base_arrivals(u):
-        return [remote(keep.at[0, t, half:half + sims], out_ref.at[:, span(other(t, False), u)], ts.at[0, t - 1], tr.at[u, t - 1], r, mate)
+        return [remote(base_s.at[0, t - 1], out_ref.at[:, span(other(t, False), u)], ts.at[0, t - 1], tr.at[u, t - 1], r, mate)
                 for t in range(1, chips)]
 
     def own_copy(u, same=True):
-        k = lax.rem(u, keep.shape[0])
-        return remote(keep.at[k, 0, half:half + sims], out_ref.at[:, span(other(0, same), u)], us.at[k], ur.at[u], r, mate)
+        k = lax.rem(u, keeps)
+        return remote(own_s.at[k], out_ref.at[:, span(other(0, same), u)], us.at[k], ur.at[u], r, mate)
 
     chunks = 8 if units % 8 == 0 else units
     many = units // chunks
@@ -226,88 +241,125 @@
     greet(line + peers)
     acc[...] = jnp.zeros_like(acc)
     tabulate(r, idx_ref, held, table, where_v, where_s, tables, ws)
-    for cp in [weights] + [cp for u in range(min(2, units)) for cp in loads(u) + [proj_load(u)]]:
+    for cp in [weights] + [cp for u in range(min(start + 2, units)) for cp in loads(u)] + [proj_load(u) for u in range(min(2, units))]:
         cp.start()
-    drain = spread(n_row, n_col, r, c, peers, ready, p_ref, table, where_v, where_s, rows_v, own, land, mine, gather, s5, r5, s6, r6)
-    weights.wait()
-
-    def sum_chip(u):
+    arrive, drain = spread(n_row, n_col, r, c, peers, ready, p_ref, table, where_v, where_s, rows_v, own, land, mine, gather, s5, r5, s6, r6)
+
+    def sum_chip(u, halves=(0, 1)):
+        k, q, e = lax.rem(u, lent), lax.rem(u, near_r.shape[0]), lax.rem(u, keeps)
+        away = far_copies(u) if len(halves) == 2 else far_half(u, halves[0])
+        base = base_copies(u) if halves[-1] == 1 else []
+        for t in list(range(1, chips)) + [0]:
+            for h in halves:
+                b = h * half
+                lo = keep[e, t, b:b + quad] + near_r[q, t, b + quad:b + half]
+                hi = keep[e, t, b + quad:b + half] + near_r[q, t, b:b + quad]
+                if t > 0:
+                    far_s[k, t - 1, b:b + quad] = lo.astype(jnp.bfloat16)
+                    far_s[k, t - 1, b + quad:b + half] = hi.astype(jnp.bfloat16)
+                    out_ref[h * hs:(h + 1) * hs, span(other(t, True), u)] = lo[:hs]
+                    base_s[e, t - 1, h * hs:(h + 1) * hs] = hi[:hs]
+                else:
+                    keep[e, 0, b:b + quad] = lo
+                    keep[e, 0, b + quad:b + half] = hi
+            if t > 0:
+                away[t - 1].start()
+                if base:
+                    base[t - 1].start()
+
+    def multiply(u, halves=(0, 1)):
+        n, k, e = lax.rem(u, stock), lax.rem(u, hold), lax.rem(u, keeps)
+        for o in range(2):
+            for t in range(chips):
+                value = lax.dot_general(p_ref[halves[0] * half:(halves[-1] + 1) * half, :], obs_v[n, o * chips + t], NT, preferred_element_type=jnp.float32)
+                for i, h in enumerate(halves):
+                    first = value[i * half:i * half + hs] + pri_v[n, o * chips + t, h * hs:(h + 1) * hs]
+                    rest, b = value[i * half + hs:(i + 1) * half], h * half
+                    if o == 0:
+                        near_s[k, t, b:b + hs] = first
+                        near_s[k, t, b + hs:b + half] = rest
+                    else:
+                        keep[e, t, b:b + hs] = first
+                        keep[e, t, b + hs:b + half] = rest
+            if o == 0:
+                (near_copy(u) if len(halves) == 2 else near_half(u, halves[0])).start()
+
+    def sum_next(u):
         near_copy(u).wait_recv()
 
-        @pl.when(u >= far_s.shape[0])
-        def _():
-            for cp in far_copies(u - far_s.shape[0]):
+        @pl.when(u >= lent + start)
+        def _():
+            for cp in far_copies(u - lent):
                 cp.wait_send()
 
-        k, q, e = lax.rem(u, far_s.shape[0]), lax.rem(u, near_r.shape[0]), lax.rem(u, keep.shape[0])
-        away, base = far_copies(u), base_copies(u)
-        for t in list(range(1, chips)) + [0]:
-            lo = keep[e, t, :half] + near_r[q, t, half:]
-            hi = keep[e, t, half:] + near_r[q, t, :half]
-            if t > 0:
-                far_s[k, t - 1, :half] = lo.astype(jnp.bfloat16)
-                far_s[k, t - 1, half:] = hi.astype(jnp.bfloat16)
-                away[t - 1].start()
-                out_ref[:, span(other(t, True), u)] = lo[:sims]
-                keep[e, t, half:half + sims] = hi[:sims]
-                base[t - 1].start()
-            else:
-                keep[e, 0, :half] = lo
-                keep[e, 0, half:] = hi
-
-    def multiply(u):
-        n, k, e = lax.rem(u, IN), lax.rem(u, near_s.shape[0]), lax.rem(u, keep.shape[0])
+        if start:
+            @pl.when((u >= lent) & (u < lent + start))
+            def _():
+                for h in range(2):
+                    for cp in far_half(u - lent, h):
+                        cp.wait_send()
+
+        sum_chip(u)
+
+    def multiply_next(u):
         for cp in loads(u):
             cp.wait()
 
-        @pl.when(u >= near_s.shape[0])
-        def _():
-            near_copy(u - near_s.shape[0]).wait_send()
-
-        @pl.when(u >= keep.shape[0])
-        def _():
-            for cp in base_copies(u - keep.shape[0]) + [own_copy(u - keep.shape[0])]:
+        @pl.when(u >= hold + start)
+        def _():
+            near_copy(u - hold).wait_send()
+
+        if start:
+            @pl.when((u >= hold) & (u < hold + start))
+            def _():
+                for h in range(2):
+                    near_half(u - hold, h).wait_send()
+
+        @pl.when(u >= keeps)
+        def _():
+            for cp in base_copies(u - keeps) + [own_copy(u - keeps)]:
                 cp.wait_send()
 
-        for o in range(2):
-            for t in range(chips):
-                value = lax.dot_general(p_ref[...], obs_v[n, o * chips + t], NT, preferred_element_type=jnp.float32)
-                first = value[:sims] + pri_v[n, o * chips + t]
-                if o == 0:
-                    near_s[k, t, :sims] = first
-                    near_s[k, t, sims:] = value[sims:]
-                else:
-                    keep[e, t, :sims] = first
-                    keep[e, t, sims:] = value[sims:]
-            if o == 0:
-                near_copy(u).start()
+        multiply(u)
 
     def project(u):
-        for cp in far_copies(u):
-            cp.wait_recv()
-        q, e, n = lax.rem(u, far_r.shape[0]), lax.rem(u, keep.shape[0]), lax.rem(u, IN)
+        @pl.when(u >= start)
+        def _():
+            for cp in far_copies(u):
+                cp.wait_recv()
+
+        if start:
+            @pl.when(u < start)
+            def _():
+                for h in range(2):
+                    for cp in far_half(u, h):
+                        cp.wait_recv()
+
+        q, e, n = lax.rem(u, far_r.shape[0]), lax.rem(u, keeps), lax.rem(u, proj_v.shape[0])
         wide = size // LANES
         weight = jnp.concatenate([apod_ref[pl.ds((c * units + u) * wide + i, 1), :] for i in range(wide)], axis=1)
         for h in range(2):
-            for b in range(chips):
-                at = slice((h * chips + b) * sims, (h * chips + b + 1) * sims)
-                total, last = keep[e, 0, at], None
-                for t in range(1, chips):
-                    s = h * chips + (b + t) % chips
-                    term = far_r[q, t - 1, s * sims:(s + 1) * sims].astype(jnp.float32)
-                    if b > 0 and t == chips - b:
-                        last = term
+            part = slice(h * hs, (h + 1) * hs)
+            for f in range(2):
+                for b in range(chips):
+                    at = slice(h * half + (f * chips + b) * hs, h * half + (f * chips + b + 1) * hs)
+                    total, last = keep[e, 0, at], None
+                    for t in range(1, chips):
+                        s = h * half + (f * chips + (b + t) % chips) * hs
+                        term = far_r[q, t - 1, s:s + hs].astype(jnp.float32)
+                        if b > 0 and t == chips - b:
+                            last = term
+                        else:
+                            total = total + term
+                    if b > 0:
+                        g_s[(b - 1) * 2 + f, u, part] = total.astype(jnp.bfloat16)
+                        total = total + last
+                    elif f == 0:
+                        out_ref[part, span(c, u)] = total
                     else:
-                        total = total + term
-                if b > 0:
-                    g_s[(b - 1) * 2 + h, u] = total.astype(jnp.bfloat16)
-                    total = total + last
-                elif h == 0:
-                    out_ref[:, span(c, u)] = total
-                else:
-                    keep[e, 0, half:half + sims] = total
-                    own_copy(u).start()
-                w_v[at] = (weight * total).astype(jnp.bfloat16)
+                        own_s[e, part] = total
+                    w_v[at] = (weight * total).astype(jnp.bfloat16)
+        own_copy(u).start()
         proj_load(u).wait()
         tile = min(512, prows)
         for j in range(0, prows, tile):
@@ -325,13 +377,13 @@
             for cp in loads(g + 2):
                 cp.start()
 
-        @pl.when((g >= D2) & (g < units + D2))
-        def _():
-            sum_chip(g - D2)
+        @pl.when((g >= start + D2) & (g < units + D2))
+        def _():
+            sum_next(g - D2)
 
         @pl.when(g < units)
         def _():
-            multiply(g)
+            multiply_next(g)
 
         @pl.when(g >= D3)
         def _():
@@ -345,14 +397,26 @@
 
         return carry
 
-    lax.fori_loop(0, units + D3, step, 0)
-
-    hs, pb = sims // 2, prows // n_row
+    for h in range(2):
+        arrive(h)
+        for i in range(start + 1):
+            if i < start:
+                if h == 0:
+                    for cp in loads(i):
+                        cp.wait()
+                multiply(i, (h,))
+            if 0 < i:
+                near_half(i - 1, h).wait_recv()
+                sum_chip(i - 1, (h,))
+    weights.wait()
+    lax.fori_loop(start, units + D3, step, 0)
+
+    pb = prows // n_row
     pieces = [(t, h) for t in reversed(range(chips)) for h in range(2)]
 
     def swap_copy(i):
         t, h = pieces[i]
-        return remote(acc.at[half + t * sims + h * hs:half + t * sims + (h + 1) * hs], swap.at[i], s1.at[i], r1.at[i], r, mate)
+        return remote(acc.at[h * half + quad + t * hs:h * half + quad + (t + 1) * hs], swap.at[i], s1.at[i], r1.at[i], r, mate)
 
     def y_copy(i):
         return remote(fb.at[i, 1 - low], yb.at[i], s2.at[i], r2.at[i], beside, c)
@@ -371,7 +435,7 @@
         t, h = pieces[i]
         swap_copy(i).wait_recv()
         for k in range(n_row):
-            fb[i, k % 2, k // 2] = acc[t * sims + h * hs:t * sims + (h + 1) * hs, k * pb:(k + 1) * pb] + swap[i, :, k * pb:(k + 1) * pb]
+            fb[i, k % 2, k // 2] = acc[h * half + t * hs:h * half + (t + 1) * hs, k * pb:(k + 1) * pb] + swap[i, :, k * pb:(k + 1) * pb]
         y_copy(i).start()
     for i in every:
         y_copy(i).wait_recv()
@@ -451,6 +515,8 @@
     back = 2 * (chips - 1)
     chunks = 8 if units % 8 == 0 else units
     n_keep, n_far = D3 + 2, 2 * (D3 - D2) + 2
+    start = min(EARLY, units // 4)
+    hold, lent, stock = max(2, start + 1), max(SENDS, start), max(3, start + 2)
     vmem, anywhere = pl.BlockSpec(memory_space=pltpu.VMEM), pl.BlockSpec(memory_space=pltpu.HBM)
     dma, bf16, f32 = pltpu.SemaphoreType.DMA, jnp.bfloat16, jnp.float32
     return pl.pallas_call(
@@ -470,13 +536,15 @@
             pltpu.VMEM((n_row, halves, sims // halves, part), bf16),
             pltpu.VMEM((all_sims, depth), bf16),
             pltpu.VMEM((rows // LANES, LANES), f32),
-            pltpu.VMEM((IN, n_col, size, depth), bf16),
-            pltpu.VMEM((IN, n_col, sims, size), f32),
-            pltpu.VMEM((IN, prows, size), bf16),
-            pltpu.VMEM((2, chips, all_sims, size), f32),
-            pltpu.VMEM((2 * D2, chips, all_sims, size), f32),
+            pltpu.VMEM((stock, n_col, size, depth), bf16),
+            pltpu.VMEM((stock, n_col, sims, size), f32),
+            pltpu.VMEM((3, prows, size), bf16),
+            pltpu.VMEM((hold, chips, all_sims, size), f32),
+            pltpu.VMEM((hold, chips, all_sims, size), f32),
             pltpu.VMEM((n_keep, chips, all_sims, size), f32),
-            pltpu.VMEM((SENDS, chips - 1, all_sims, size), bf16),
+            pltpu.VMEM((n_keep, chips - 1, sims, size), f32),
+            pltpu.VMEM((n_keep, sims, size), f32),
+            pltpu.VMEM((lent, chips - 1, all_sims, size), bf16),
             pltpu.VMEM((n_far, chips - 1, all_sims, size), bf16),
             pltpu.VMEM((all_sims, size), bf16),
             pltpu.VMEM((all_sims, prows), f32),
@@ -490,8 +558,10 @@
             pltpu.VMEM((pieces, hs, pb), f32),
             pltpu.VMEM((pieces, hs, pb), f32),
             pltpu.SemaphoreType.REGULAR, dma((rows // width,)), dma, dma((halves, n_row - 1)), dma((halves, n_row - 1)), dma((halves, n_row)), dma((halves, n_row)),
-            dma, dma((IN, n_col)), dma((IN, n_col)), dma((IN,)), dma((2,)), dma((2 * D2,)),
-            dma((SENDS, chips - 1)), dma((n_far, chips - 1)),
+            dma, dma((stock, n_col)), dma((stock, n_col)), dma((3,)), dma((hold,)), dma((hold,)),
+            dma((max(1, start), 2)), dma((max(1, start), 2)),
+            dma((lent, chips - 1)), dma((n_far, chips - 1)),
+            dma((max(1, start), 2, chips - 1)), dma((max(1, start), 2, chips - 1)),
             dma((n_keep, chips - 1)), dma((units, chips - 1)), dma((n_keep,)), dma((units,)),
             dma((chunks, back)), dma((chunks, back)),
             dma((pieces,)), dma((pieces,)), dma((pieces,)), dma((pieces,)),

time: 134 us -> 133 us (level)
  Pallas kernels: 133 us -> 131 us
    pallas_call x1, Pallas kernels: 130 us -> 128 us  [stream(): pl.pallas_call(functools.partial(stream_kernel, n_row, n_col, units), in_...]
where the time goes in v4:
time: 133 us
  Pallas kernels  131 us (98%)
    pallas_call x1, Pallas kernels, stream(): pl.pallas_call(functools.partial(stream_kernel, n_row, n_col, units), in_...  128 us
    pallas_call x1, Pallas kernels, emit(): pl.pallas_call(emit_kernel, out_shape=[jax.ShapeDtypeStruct(x.shape, x.dt...  2.77 us

profile of v4, /device:TPU:0, one launch (start us, length us, event | category | flops | bytes accessed | tf_op | source)
XLA Modules:
  0.0 132.5 jit_solution(13184189248674294944)
XLA Ops:
  0.6 0.0 copy-start
  0.6 0.7 copy-done
  1.3 128.4 %stream.1 = (f32[64,24576]{1,0:T(8,128)S(1)}, f32[64,256]{1,0:T(8,128)S(1)}) custom-call(s32[16,128]{1,0:T(8,128)S(1)} %bitcast.6, bf16[64,24576]{1,0:T(8,128)(2,1)} %bitcast.8, f32[192,128]{1,0:T(8,128)} %bitcast.9, bf16[24576,512]{1,0:T(8,128)(2,1)} %obs.1, f32[64,24576]{1,0:T(8,128)} %bitcast.7, bf16[2048,6144]{1,0:T(8,128)(2,1)} %proj.1), custom_call_target="tpu_custom_call" | custom-call | tf_op jit(solution)/shard_map/stream/pallas_call | solution.py:522
  129.8 2.8 %emit.1 = (f32[64,24576]{1,0:T(8,128)}, f32[64,256]{1,0:T(8,128)}) custom-call(f32[64,24576]{1,0:T(8,128)S(1)} %get-tuple-element.6.out_ref, f32[64,256]{1,0:T(8,128)S(1)} %get-tuple-element.7.pout_ref), custom_call_target="tpu_custom_call" | custom-call | tf_op jit(solution)/shard_map/emit/pallas_call | solution.py:588
Async XLA Ops:
  0.6 0.7 copy-start

commit v5 on v4

--- a/solution.py
+++ b/solution.py
@@ -15,6 +15,7 @@
 SENDS, EARLY = 3, 2
 LIMIT = 46 * 1024 * 1024
 LANES = 128
+EMIT_ROWS, EMIT_COLS = 2, 1
 AHEAD = 3
 
 
@@ -74,7 +75,6 @@
         for t in range(tiles):
             for j in range(LANES):
                 rows_v[t * LANES + j:t * LANES + j + 1, :] = table[pl.ds(where_s[k * tiles + t, j], 1), :]
-        for t in range(tiles):
             flat = lax.dot_general(turn, rows_v[t * LANES:(t + 1) * LANES, :].astype(own.dtype), NT, preferred_element_type=jnp.float32)
             which = where_v[pl.ds(k * tiles + t, 1), :]
             total = jnp.zeros((sims, LANES), jnp.float32)
@@ -573,10 +573,12 @@
 
 
 def emit_kernel(out_ref, pout_ref, out, pout, sem):
-    rows = math.gcd(out_ref.shape[0], 8)
+    rows, wide = out_ref.shape[0] // EMIT_ROWS, out_ref.shape[1] // EMIT_COLS
     copies = [pltpu.make_async_copy(pout_ref, pout, sem.at[0])]
-    for i in range(out_ref.shape[0] // rows):
-        copies.append(pltpu.make_async_copy(out_ref.at[i * rows:(i + 1) * rows], out.at[i * rows:(i + 1) * rows], sem.at[i + 1]))
+    for i in range(EMIT_ROWS):
+        for j in range(EMIT_COLS):
+            at = (slice(i * rows, (i + 1) * rows), slice(j * wide, (j + 1) * wide))
+            copies.append(pltpu.make_async_copy(out_ref.at[at], out.at[at], sem.at[len(copies)]))
     for cp in copies:
         cp.start()
     for cp in copies:
@@ -590,7 +592,7 @@
         out_shape=[jax.ShapeDtypeStruct(x.shape, x.dtype) for x in (out, pout)],
         in_specs=[vmem] * 2,
         out_specs=[hbm] * 2,
-        scratch_shapes=[pltpu.SemaphoreType.DMA((out.shape[0] // math.gcd(out.shape[0], 8) + 1,))],
+        scratch_shapes=[pltpu.SemaphoreType.DMA((EMIT_ROWS * EMIT_COLS + 1,))],
         compiler_params=pltpu.CompilerParams(vmem_limit_bytes=8 * 1024 * 1024),
         name="emit",
     )(out, pout)

time: 133 us -> 132 us (level)
  no operation moved by 1% of the time
where the time goes in v5:
time: 132 us
  Pallas kernels  131 us (99%)
    pallas_call x1, Pallas kernels, stream(): pl.pallas_call(functools.partial(stream_kernel, n_row, n_col, units), in_...  128 us
    pallas_call x1, Pallas kernels, emit(): pl.pallas_call(emit_kernel, out_shape=[jax.ShapeDtypeStruct(x.shape, x.dt...  2.75 us

profile of v5, /device:TPU:0, one launch (start us, length us, event | category | flops | bytes accessed | tf_op | source)
XLA Modules:
  0.0 132.0 jit_solution(359029972535974713)
XLA Ops:
  0.6 0.0 copy-start
  0.6 0.7 copy-done
  1.3 128.0 %stream.1 = (f32[64,24576]{1,0:T(8,128)S(1)}, f32[64,256]{1,0:T(8,128)S(1)}) custom-call(s32[16,128]{1,0:T(8,128)S(1)} %bitcast.6, bf16[64,24576]{1,0:T(8,128)(2,1)} %bitcast.8, f32[192,128]{1,0:T(8,128)} %bitcast.9, bf16[24576,512]{1,0:T(8,128)(2,1)} %obs.1, f32[64,24576]{1,0:T(8,128)} %bitcast.7, bf16[2048,6144]{1,0:T(8,128)(2,1)} %proj.1), custom_call_target="tpu_custom_call" | custom-call | tf_op jit(solution)/shard_map/stream/pallas_call | solution.py:522
  129.3 2.7 %emit.1 = (f32[64,24576]{1,0:T(8,128)}, f32[64,256]{1,0:T(8,128)}) custom-call(f32[64,24576]{1,0:T(8,128)S(1)} %get-tuple-element.6.out_ref, f32[64,256]{1,0:T(8,128)S(1)} %get-tuple-element.7.pout_ref), custom_call_target="tpu_custom_call" | custom-call | tf_op jit(solution)/shard_map/emit/pallas_call | solution.py:590
Async XLA Ops:
  0.6 0.7 copy-start
